TPU v7x, 512 devices: a whole 4x8x8 slice. The times are simulated.
512 devices in a mesh: ctx: 64 (over z, y_lo, core), fsdp: 8 (over y_hi, x).
Axes of the slice: x: 4, y: 8 (y_hi: 2, y_lo: 4; y = y_hi * 4 + y_lo), z: 8, core: 2. Of those that a mesh axis runs over, the one named last changes fastest.
Arguments:
- tokens: bfloat16 [8192, 4096], P('ctx', 'fsdp'), may hold values from -130 to 130, as said below
- w_query: bfloat16 [4096, 4096], P('ctx', 'fsdp'), may hold values from -0.09375 to 0.09375
- key_matrix: bfloat16 [4096, 1024], P('ctx', 'fsdp'), may hold values from -0.09375 to 0.09375
- value_matrix: bfloat16 [4096, 1024], P('ctx', 'fsdp'), may hold values from -0.09375 to 0.09375
- w_out: bfloat16 [4096, 4096], P('fsdp', 'ctx'), may hold values from -0.75 to 0.75
Outputs:
- mixed: bfloat16 [8192, 4096], P('ctx', 'fsdp')
Inputs may be any that keep to these rules, and one draw needn't show every extreme that they name: `tokens`: no structure of the entries is promised.
All inputs are finite; a program needn't handle non-finite values.
Results may differ from a plain program's by a relative error of at most 0.014.
The roundings to bfloat16 on the way count: a program that leaves them out, or rounds other values in their place, can miss the bound.
Values may be sent and summed in bfloat16 or wider, within the bound.
A program may use at most 64 MiB of HBM per device.

v0:
```python
import math

import jax
import jax.numpy as jnp
from jax import lax
from jax.sharding import PartitionSpec as P

HEAD_SIZE = 128


def rotate_heads(values, positions):
    tok_count = values.shape[0]
    head_count = values.shape[1] // HEAD_SIZE
    half_dim = HEAD_SIZE // 2
    inverse_freq = jnp.power(
        jnp.float32(500000.0), -jnp.arange(half_dim, dtype=jnp.float32) * 2.0 / HEAD_SIZE
    )
    angles = positions.astype(jnp.float32)[:, None] * inverse_freq[None, :]
    cosine = jnp.cos(angles)[:, None, :]
    sine_table = jnp.sin(angles)[:, None, :]
    shaped = values.reshape(tok_count, head_count, HEAD_SIZE)
    first_half = shaped[:, :, :half_dim]
    second = shaped[:, :, half_dim:]
    turned = jnp.concatenate(
        [first_half * cosine - second * sine_table, second * cosine + first_half * sine_table],
        axis=2,
    )
    return turned.reshape(tok_count, head_count * HEAD_SIZE).astype(jnp.bfloat16)


def body(tokens, w_query, key_matrix, value_matrix, w_out):
    features = lax.all_gather(tokens, "fsdp", axis=1, tiled=True)
    tok_count = features.shape[0]
    positions = lax.axis_index("ctx") * tok_count + jnp.arange(tok_count, dtype=jnp.int32)

    def add_rows(weight_piece):
        return jnp.dot(features, weight_piece, preferred_element_type=jnp.float32)

    query_sum = add_rows(lax.all_gather(w_query, "ctx", axis=0, tiled=True))
    key_sum = add_rows(lax.all_gather(key_matrix, "ctx", axis=0, tiled=True))
    value_sum = add_rows(lax.all_gather(value_matrix, "ctx", axis=0, tiled=True))
    queries = rotate_heads(query_sum, positions)
    projected_keys = rotate_heads(key_sum, positions)
    projected_values = value_sum.astype(jnp.bfloat16)
    kv_heads = projected_keys.shape[1] // HEAD_SIZE
    queries_per_group = queries.shape[1] // projected_keys.shape[1]
    stacked = (
        queries.reshape(tok_count, kv_heads, queries_per_group, HEAD_SIZE)
        .transpose(1, 2, 0, 3)
        .reshape(kv_heads, queries_per_group * tok_count, HEAD_SIZE)
    )
    query_pos = jnp.tile(positions, queries_per_group)
    score_scale = 1.0 / math.sqrt(HEAD_SIZE)

    def update(attn_state, key_block, value_block, key_start):
        row_max, row_total, accum = attn_state
        block_rows = key_block.shape[0]
        key_heads = key_block.reshape(block_rows, kv_heads, HEAD_SIZE)
        value_heads = value_block.reshape(block_rows, kv_heads, HEAD_SIZE)
        scores = (
            jnp.einsum("gqd,kgd->gqk", stacked, key_heads, preferred_element_type=jnp.float32)
            * score_scale
        )
        key_pos = key_start + jnp.arange(block_rows, dtype=jnp.int32)
        allowed = (key_pos[None, :] <= query_pos[:, None])[None]
        masked = jnp.where(allowed, scores, jnp.float32(-1e30))
        new_max = jnp.maximum(row_max, jnp.max(masked, axis=2))
        exp_weights = jnp.where(allowed, jnp.exp(masked - new_max[:, :, None]), jnp.float32(0.0))
        factor = jnp.exp(row_max - new_max)
        row_total = row_total * factor + jnp.sum(exp_weights, axis=2)
        accum = accum * factor[:, :, None] + jnp.einsum(
            "gqk,kgd->gqd",
            exp_weights.astype(jnp.bfloat16),
            value_heads,
            preferred_element_type=jnp.float32,
        )
        return (new_max, row_total, accum)

    query_rows = queries_per_group * tok_count
    initial = (
        jnp.full((kv_heads, query_rows), -1e30, jnp.float32),
        jnp.zeros((kv_heads, query_rows), jnp.float32),
        jnp.zeros((kv_heads, query_rows, HEAD_SIZE), jnp.float32),
    )
    key_piece = lax.all_gather(projected_keys, "ctx", axis=0, tiled=True)
    value_piece = lax.all_gather(projected_values, "ctx", axis=0, tiled=True)
    block_rows = min(tok_count, key_piece.shape[0])
    block_count = key_piece.shape[0] // block_rows

    def advance(block_index, carried):
        key_start = block_index * block_rows
        key_block = lax.dynamic_slice_in_dim(key_piece, block_index * block_rows, block_rows, 0)
        value_block = lax.dynamic_slice_in_dim(value_piece, block_index * block_rows, block_rows, 0)
        return update(carried, key_block, value_block, key_start)

    row_max, row_total, accum = lax.fori_loop(0, block_count, advance, initial)
    normed = accum / row_total[:, :, None]
    attn_out = (
        normed.reshape(kv_heads, queries_per_group, tok_count, HEAD_SIZE)
        .transpose(2, 0, 1, 3)
        .reshape(tok_count, kv_heads * queries_per_group * HEAD_SIZE)
        .astype(jnp.bfloat16)
    )
    partial_out = jnp.dot(
        attn_out,
        lax.all_gather(w_out, "ctx", axis=1, tiled=True),
        preferred_element_type=jnp.float32,
    )
    return lax.psum_scatter(
        partial_out.astype(jnp.bfloat16), "fsdp", scatter_dimension=1, tiled=True
    )


def solution(mesh):
    in_specs = (
        P("ctx", "fsdp"),
        P("ctx", "fsdp"),
        P("ctx", "fsdp"),
        P("ctx", "fsdp"),
        P("fsdp", "ctx"),
    )
    out_specs = P("ctx", "fsdp")
    return jax.shard_map(body, mesh=mesh, in_specs=in_specs, out_specs=out_specs, check_vma=False)
```

profile of v0, /device:TPU:1, one launch (start us, length us, event | category | flops | bytes accessed | tf_op | source)
XLA Modules:
  0.0 911.5 jit_solution(4390556370071659170)
XLA Ops:
  9.4 67.8 %all-gather.9.cloned.1.call-done = bf16[128,4096]{1,0:T(8,128)(2,1)} async-done(((bf16[128,512]{1,0:T(8,128)(2,1)}), bf16[128,4096]{1,0:T(8,128)(2,1)}) %all-gather.9.cloned.1.call-update) | async-done | bytes 1048592 | tf_op jit(solution)/shard_map/all_gather | solution.py:32
  77.2 120.3 %all-gather.11.cloned.1.call-done = bf16[4096,128]{1,0:T(8,128)(2,1)} async-done(((bf16[64,128]{1,0:T(8,128)(2,1)}), bf16[4096,128]{1,0:T(8,128)(2,1)}) %all-gather.11.cloned.1.call-update) | async-done | bytes 1048592 | tf_op jit(solution)/shard_map/all_gather | solution.py:40
  197.5 2.1 convolution_bitcast_fusion.1
  200.5 114.5 %all-gather.15.cloned.1.call-done = bf16[4096,128]{1,0:T(8,128)(2,1)} async-done(((bf16[64,128]{1,0:T(8,128)(2,1)}), bf16[4096,128]{1,0:T(8,128)(2,1)}) %all-gather.15.cloned.1.call-update) | async-done | bytes 1048592 | tf_op jit(solution)/shard_map/all_gather | solution.py:41
  315.0 2.6 convolution_convert_fusion.1
  318.7 116.0 %all-gather.13.cloned.1.call-done = bf16[4096,512]{1,0:T(8,128)(2,1)} async-done(((bf16[64,512]{1,0:T(8,128)(2,1)}), bf16[4096,512]{1,0:T(8,128)(2,1)}) %all-gather.13.cloned.1.call-update) | async-done | bytes 4194320 | tf_op jit(solution)/shard_map/all_gather | solution.py:39
  434.7 2.9 fusion.33
  438.2 111.7 %all-gather.21.cloned.1.call-done = bf16[8192,1,128]{0,2,1:T(8,128)(2,1)} async-done(((bf16[128,1,128]{0,2,1:T(8,128)(2,1)}), bf16[8192,1,128]{0,2,1:T(8,128)(2,1)}) %all-gather.21.cloned.1.call-update) | async-done | bytes 2097168 | tf_op jit(solution)/shard_map/all_gather | solution.py:85
  549.9 116.5 %all-gather.17.cloned.1.call-done = bf16[8192,128]{1,0:T(8,128)(2,1)} async-done(((bf16[128,128]{1,0:T(8,128)(2,1)}), bf16[8192,128]{1,0:T(8,128)(2,1)}) %all-gather.17.cloned.1.call-update) | async-done | bytes 2097168 | tf_op jit(solution)/shard_map/all_gather | solution.py:86
  666.3 145.2 %while.18 = (s32[]{:T(128)}, f32[1,512]{1,0:T(1,128)S(1)}, f32[1,512]{1,0:T(1,128)S(1)}, f32[1,512,128]{2,1,0:T(8,128)S(1)}, bf16[8192,128]{0,1:T(8,128)(2,1)}, ...) while((s32[]{:T(128)}, f32[1,512]{1,0:T(1,128)S(1)}, ...), condition=%wide.region_3.4_spmd.clone, body=%wide.region_0.3_spmd.clone.sunk | while | flops 34540164 | bytes 1551035 | solution.py:96
  687.9 1.1 fusion.55
  701.5 1.1 fusion.55
  708.3 1.1 fusion.55
  722.0 1.1 fusion.55
  733.3 1.1 fusion.55
  735.6 1.1 fusion.55
  749.2 1.1 fusion.55
  756.0 1.1 fusion.55
  771.9 1.1 fusion.55
  776.4 1.1 fusion.55
  781.0 1.1 fusion.55
  783.2 1.1 fusion.55
  811.9 4.7 convolution_convert_fusion
  816.6 88.1 %reduce-scatter.2.cloned.1.call-done = bf16[128,512]{1,0:T(8,128)(2,1)} async-done(((bf16[128,4096]{1,0:T(8,128)(2,1)}), bf16[128,512]{1,0:T(8,128)(2,1)}) %reduce-scatter.2.cloned.1.call-update) | async-done | bytes 131088 | tf_op jit(solution)/shard_map/reduce_scatter | solution.py:109
  (534 shorter events, 133.6 us)
Async XLA Ops:
  6.5 70.7 %all-gather.9.cloned.1.call-start = ((), (), s32[]{:S(2)}) async-start(), calls=%async_computation.1 | async-start | bytes 1179648 | tf_op jit(solution)/shard_map/all_gather | solution.py:32
  7.3 190.3 %all-gather.11.cloned.1.call-start = ((), (), s32[]{:S(2)}) async-start(), calls=%async_computation.2 | async-start | bytes 1064960 | tf_op jit(solution)/shard_map/all_gather | solution.py:40
  8.0 307.0 %all-gather.15.cloned.1.call-start = ((), (), s32[]{:S(2)}) async-start(), calls=%async_computation.4 | async-start | bytes 1064960 | tf_op jit(solution)/shard_map/all_gather | solution.py:41
  8.7 425.9 %all-gather.13.cloned.1.call-start = ((), (), s32[]{:S(2)}) async-start(), calls=%async_computation.3 | async-start | bytes 4259840 | tf_op jit(solution)/shard_map/all_gather | solution.py:39
  9.3 540.5 %all-gather.21.cloned.1.call-start = ((), (), s32[]{:S(2)}) async-start(), calls=%async_computation.8 | async-start | bytes 2129920 | tf_op jit(solution)/shard_map/all_gather | solution.py:85
  77.2 357.5 %copy-start = (bf16[128,4096]{1,0:T(8,128)(2,1)S(1)}, bf16[128,4096]{1,0:T(8,128)(2,1)}, u32[]{:S(2)}) copy-start(bf16[128,4096]{1,0:T(8,128)(2,1)} %all-gather.9.cloned.1.call-done) | copy-start | bytes 3145732
  200.4 465.9 %all-gather.17.cloned.1.call-start = ((), (), s32[]{:S(2)}) async-start(), calls=%async_computation.5 | async-start | bytes 2129920 | tf_op jit(solution)/shard_map/all_gather | solution.py:86
  317.6 494.3 %all-gather.19.cloned.1.call-start = ((), (), s32[]{:S(2)}) async-start(), calls=%async_computation.6 | async-start | bytes 4259840 | tf_op jit(solution)/shard_map/all_gather | solution.py:106
  318.3 586.4 %reduce-scatter.2.cloned.1.call-start = ((), (), s32[]{:S(2)}) async-start(), calls=%async_computation.7 | async-start | bytes 1179648 | tf_op jit(solution)/shard_map/reduce_scatter | solution.py:109
Sparse Core Ops, SparseCore 0:
  10.4 66.7 all-gather.8
  79.4 118.1 all-gather.10
  199.7 115.2 all-gather.14
  317.0 117.6 all-gather.12
  436.6 113.2 all-gather.20
  551.9 114.4 all-gather.16
  668.5 117.7 all-gather.18
  816.7 87.9 reduce-scatter.1
where the time goes:
time: 921 us; the launch traced here: 912 us
  waiting for transfers between devices  738 us (80%)
  matrix products  144 us (16%)
  between operations  13.6 us (1%)
  other arithmetic  10.8 us (1%)
    all_gather x1, waiting for transfers between devices, body(): key_sum = add_rows(lax.all_gather(key_matrix, 'ctx', axis=0, tiled=True))  120 us
    all_gather x1, waiting for transfers between devices, body(): value_piece = lax.all_gather(projected_values, 'ctx', axis=0, tiled=True)  116 us
    all_gather x1, waiting for transfers between devices, body(): query_sum = add_rows(lax.all_gather(w_query, 'ctx', axis=0, tiled=True))  116 us
    all_gather x1, waiting for transfers between devices, body(): lax.all_gather(value_matrix, 'ctx', axis=0, tiled=True)  114 us
    all_gather x1, waiting for transfers between devices, body(): key_piece = lax.all_gather(projected_keys, 'ctx', axis=0, tiled=True)  112 us
    reduce_scatter x1, waiting for transfers between devices, body(): lax.psum_scatter(partial_out.astype(jnp.bfloat16), 'fsdp', scatter_dimens...  88.1 us
    dot_general x64, matrix products, update(): jnp.einsum('gqk,kgd->gqd', exp_weights.astype(jnp.bfloat16), value_heads,...  68.1 us
    all_gather x1, waiting for transfers between devices, body(): features = lax.all_gather(tokens, 'fsdp', axis=1, tiled=True)  67.8 us
  transfers between devices with their start and end apart: 8, of which 7 were waited for; matrix products, arithmetic and copies ran while one was open for 16% of the time, Pallas kernels for 0%

commit v1 on v0

v1 whole, which is shorter than its diff:
```python
import functools
import math

import jax
import jax.numpy as jnp
import numpy as np
from jax import lax
from jax.experimental import pallas as pl
from jax.experimental.pallas import tpu as pltpu
from jax.sharding import PartitionSpec as P

MESH = pl.DeviceIdType.MESH
HEAD = 128
HEADS = 4
NZ, NY = 8, 4
TOK = 128
SCALE2 = math.log2(math.e) / math.sqrt(HEAD)
REACH = ((4, 4, 3, 3), (3, 3, 4, 4))
W, KV, WO = 0, 1, 2


def kernel(
    tok, wq, wk, wv, wo, invf, out,
    xbuf, wbuf, kvbuf, wobuf, wo_in, qbuf, proj, mbuf, lbuf, acc, abuf, pbuf, rbuf, sbuf, ybuf,
    local, zsend, ysend, bsend, zrecv, brecv, tsend, trecv, rsend, rrecv, hsend, hrecv,
):
    c = lax.axis_index("ctx")
    f = lax.axis_index("fsdp")
    k = c % 2
    y = (c // 2) % NY
    z = c // (2 * NY)
    x = f % 4
    yh = f // 4

    def at(zz, yy, kk):
        return ((zz * NY + yy) * 2 + kk, f)

    def up(d, n):
        return (z + (n if d == 0 else NZ - n)) % NZ

    def yo(dy):
        return (y + dy) % NY

    bufs = (wbuf, kvbuf, wobuf)

    def zcopy(g, d, step, dy):
        zz, yy = up(1 - d, step), yo(dy)
        ref = bufs[g].at[zz, yy, k]
        return pltpu.make_async_remote_copy(
            src_ref=ref, dst_ref=ref, send_sem=zsend.at[g, d, step, dy], recv_sem=zrecv.at[g, zz, yy],
            device_id=at(up(d, 1), y, k), device_id_type=MESH,
        )

    def ycopy(g, dy):
        ref = bufs[g].at[z, y, k]
        return pltpu.make_async_remote_copy(
            src_ref=ref, dst_ref=ref, send_sem=ysend.at[g, dy - 1], recv_sem=zrecv.at[g, z, y],
            device_id=at(z, yo(dy), k), device_id_type=MESH,
        )

    def bcopy(g, zz):
        ref = bufs[g].at[zz, :, k]
        return pltpu.make_async_remote_copy(
            src_ref=ref, dst_ref=ref, send_sem=bsend.at[g, zz], recv_sem=brecv.at[g, zz],
            device_id=at(z, y, 1 - k), device_id_type=MESH,
        )

    def arrived(g, zz, yy):
        ref = bufs[g].at[zz, yy, k]
        pltpu.make_async_remote_copy(
            src_ref=ref, dst_ref=ref, send_sem=zsend.at[g, 0, 0, 0], recv_sem=zrecv.at[g, zz, yy],
            device_id=at(z, y, 1 - k), device_id_type=MESH,
        ).wait_recv()

    def paired(g, zz):
        ref = bufs[g].at[zz, :, 1 - k]
        pltpu.make_async_remote_copy(
            src_ref=ref, dst_ref=ref, send_sem=bsend.at[g, zz], recv_sem=brecv.at[g, zz],
            device_id=at(z, y, 1 - k), device_id_type=MESH,
        ).wait_recv()

    def open_y(g):
        for dy in (2, 1, 3):
            ycopy(g, dy).start()

    def open_z(g):
        for d in (0, 1):
            zcopy(g, d, 0, 0).start()

    def step0(g):
        for dy in (1, 2, 3):
            arrived(g, z, yo(dy))
            for d in (0, 1):
                zcopy(g, d, 0, dy).start()
        bcopy(g, z).start()

    def step(g, s):
        for dy in range(NY):
            for d in (0, 1):
                if s <= REACH[d][dy]:
                    arrived(g, up(1 - d, s), yo(dy))
                    if s < REACH[d][dy]:
                        zcopy(g, d, s, dy).start()
        bcopy(g, up(1, s)).start()
        if s < 4:
            bcopy(g, up(0, s)).start()

    def drain(g):
        for d in (0, 1):
            for dy in range(NY):
                for s in range(REACH[d][dy]):
                    zcopy(g, d, s, dy).wait_send()
        for dy in (1, 2, 3):
            ycopy(g, dy).wait_send()
        for s in range(NZ):
            bcopy(g, up(0, s)).wait_send()

    def tcopy(n, slot, peer):
        ref = xbuf.at[slot]
        return pltpu.make_async_remote_copy(
            src_ref=ref, dst_ref=ref, send_sem=tsend.at[n], recv_sem=trecv.at[slot],
            device_id=(c, peer), device_id_type=MESH,
        )

    def tok_arrived(slot):
        tcopy(0, slot, yh * 4 + (x + 1) % 4).wait_recv()

    other = 1 - yh
    xr = yh * 4 + (x + 1) % 4
    xl = yh * 4 + (x + 3) % 4
    twin = other * 4 + x
    twin_l = other * 4 + (x + 3) % 4
    twin_r = other * 4 + (x + 1) % 4
    tokens_out = (
        (0, f, twin), (1, f, xr), (2, f, xl),
        (3, xl, xr),
        (4, twin, xr), (5, twin, xl),
        (6, twin_r, xl),
    )

    mine = wbuf.at[z, y, k]
    copies = [
        pltpu.make_async_copy(tok, xbuf.at[f], local.at[0]),
        pltpu.make_async_copy(wq, mine.at[:, pl.ds(0, 512)], local.at[1]),
        pltpu.make_async_copy(wk, mine.at[:, pl.ds(512, 128)], local.at[2]),
        pltpu.make_async_copy(wv, mine.at[:, pl.ds(640, 128)], local.at[3]),
        pltpu.make_async_copy(wo, wo_in, local.at[4]),
    ]
    for copy in copies:
        copy.start()

    barrier = pltpu.get_barrier_semaphore()
    peers = [at(up(0, 1), y, k), at(up(1, 1), y, k), at(z, y, 1 - k)]
    peers += [at(z, yo(dy), k) for dy in (1, 2, 3)]
    peers += [(c, yh * 4 + (x + dx) % 4) for dx in (1, 2, 3)]
    peers += [(c, twin)]
    for peer in peers:
        pl.semaphore_signal(barrier, inc=1, device_id=peer, device_id_type=MESH)
    for copy in copies:
        copy.wait()
    pl.semaphore_wait(barrier, len(peers))

    open_z(W)
    open_y(W)
    for n in (0, 1, 2):
        tcopy(*tokens_out[n]).start()
    wobuf[z, y, k] = wo_in[...].astype(jnp.float32).T.astype(jnp.bfloat16)
    step0(W)
    open_y(WO)

    position = (c * TOK + lax.broadcasted_iota(jnp.int32, (TOK, HEAD), 0)).astype(jnp.float32)
    angle = position * invf[...]
    cosine = jnp.cos(angle)
    lane = lax.broadcasted_iota(jnp.int32, (TOK, HEAD), 1)
    sine = jnp.sin(angle) * jnp.where(lane < HEAD // 2, -1.0, 1.0).astype(jnp.float32)

    def multiply(zz, first=False):
        paired(W, zz)
        term = jnp.dot(
            xbuf[zz], wbuf[zz].reshape(512, 768), preferred_element_type=jnp.float32
        )
        proj[...] = term if first else proj[...] + term

    step(W, 1)
    tok_arrived(xl)
    tcopy(*tokens_out[3]).start()
    tok_arrived(xr)
    tok_arrived(twin)
    tcopy(*tokens_out[4]).start()
    tcopy(*tokens_out[5]).start()
    step(W, 2)
    tok_arrived(twin_r)
    tcopy(*tokens_out[6]).start()
    tok_arrived(twin_l)
    tok_arrived(yh * 4 + (x + 2) % 4)
    step(W, 3)
    open_z(WO)
    for dy in (1, 2, 3):
        arrived(WO, z, yo(dy))
        for d in (0, 1):
            zcopy(WO, d, 0, dy).start()
    bcopy(WO, z).start()
    tok_arrived(other * 4 + (x + 2) % 4)
    multiply(z, True)
    for s in (1, 2):
        multiply(up(1, s))
        multiply(up(0, s))
    step(W, 4)
    multiply(up(1, 3))
    multiply(up(0, 3))
    multiply(up(0, 4))

    def turned(column):
        piece = proj[:, pl.ds(column, HEAD)]
        return (piece * cosine + pltpu.roll(piece, HEAD // 2, 1) * sine).astype(jnp.bfloat16)

    kvbuf[z, y, k, 0] = turned(512)
    kvbuf[z, y, k, 1] = proj[:, pl.ds(640, HEAD)].astype(jnp.bfloat16)
    open_z(KV)
    open_y(KV)
    for h in range(HEADS):
        qbuf[pl.ds(h * TOK, TOK), :] = turned(h * HEAD)

    rows = 256
    keys = NY * 2 * TOK

    def attend(zz, first=False):
        paired(KV, zz)

        def some():
            def body(i, carry):
                at_rows = pl.ds(pl.multiple_of(i * rows, rows), rows)
                key = kvbuf[zz, :, :, 0].reshape(keys, HEAD)
                value = kvbuf[zz, :, :, 1].reshape(keys, HEAD)
                score = lax.dot_general(
                    qbuf[at_rows, :], key, (((1,), (1,)), ((), ())), preferred_element_type=jnp.float32
                )
                if first:
                    key_at = lax.broadcasted_iota(jnp.int32, (rows, keys), 1)
                    query_at = (y * 2 + k) * TOK + lax.broadcasted_iota(jnp.int32, (rows, keys), 0) % TOK
                    score = jnp.where(key_at <= query_at, score, jnp.float32(-1e30))
                top = jnp.max(score, axis=1, keepdims=True)
                if first:
                    new = jnp.broadcast_to(top, (rows, HEAD))
                else:
                    old = mbuf[at_rows, :]
                    new = jnp.maximum(old, top)
                exps = jnp.exp2(score * SCALE2 - jnp.tile(new * SCALE2, (1, keys // HEAD)))
                total = jnp.sum(exps, axis=1, keepdims=True)
                summed = jnp.dot(exps.astype(jnp.bfloat16), value, preferred_element_type=jnp.float32)
                if first:
                    lbuf[at_rows, :] = jnp.broadcast_to(total, (rows, HEAD))
                    acc[at_rows, :] = summed
                else:
                    factor = jnp.exp2((old - new) * SCALE2)
                    lbuf[at_rows, :] = lbuf[at_rows, :] * factor + total
                    acc[at_rows, :] = acc[at_rows, :] * factor + summed
                mbuf[at_rows, :] = new
                return carry

            lax.fori_loop(0, HEADS * TOK // rows, body, 0)

        if first:
            some()
        else:
            pl.when(zz <= z)(some)

    step0(KV)
    step(KV, 1)
    attend(z, True)
    step(KV, 2)
    attend(up(1, 1))
    attend(up(0, 1))
    step(KV, 3)
    step(WO, 1)
    attend(up(1, 2))
    attend(up(0, 2))
    step(KV, 4)
    step(WO, 2)
    attend(up(1, 3))
    attend(up(0, 3))
    step(WO, 3)
    attend(up(0, 4))
    for h in range(HEADS):
        at_rows = pl.ds(h * TOK, TOK)
        abuf[:, pl.ds(h * HEAD, HEAD)] = (acc[at_rows, :] / lbuf[at_rows, :]).astype(jnp.bfloat16)
    step(WO, 4)
    for s in range(NZ):
        paired(WO, up(0, s))

    def block(slot):
        return lax.dot_general(
            abuf[...], wobuf[slot].reshape(512, 512), (((1,), (1,)), ((), ())),
            preferred_element_type=jnp.float32,
        ).astype(jnp.bfloat16)

    def rcopy(j, dx):
        there = (x + dx) % 4
        return pltpu.make_async_remote_copy(
            src_ref=pbuf.at[j, dx], dst_ref=rbuf.at[j, dx - 1], send_sem=rsend.at[j, dx - 1],
            recv_sem=rrecv.at[j, dx - 1], device_id=(c, yh * 4 + there), device_id_type=MESH,
        )

    for j, half in ((0, other), (1, yh)):
        for dx in (2, 1, 3, 0):
            pbuf[j, dx] = block(half * 4 + (x + dx) % 4)
            if dx:
                rcopy(j, dx).start()

    def summed_over_x(j):
        total = pbuf[j, 0].astype(jnp.float32)
        for dx in (1, 3, 2):
            rcopy(j, dx).wait_recv()
            total = total + rbuf[j, dx - 1].astype(jnp.float32)
        return total

    swap = pltpu.make_async_remote_copy(
        src_ref=sbuf, dst_ref=ybuf, send_sem=hsend.at[0], recv_sem=hrecv.at[0],
        device_id=(c, twin), device_id_type=MESH,
    )
    sbuf[...] = summed_over_x(0).astype(jnp.bfloat16)
    swap.start()
    proj[:, pl.ds(0, 512)] = summed_over_x(1)
    for g in (W, KV, WO):
        drain(g)
    for entry in tokens_out:
        tcopy(*entry).wait_send()
    for j in (0, 1):
        for dx in (1, 2, 3):
            rcopy(j, dx).wait_send()
    swap.wait()
    out[...] = (proj[:, pl.ds(0, 512)] + ybuf[...].astype(jnp.float32)).astype(jnp.bfloat16)


def body(tokens, w_query, key_matrix, value_matrix, w_out):
    half = HEAD // 2
    inverse_freq = np.power(
        np.float32(500000.0), -np.arange(half, dtype=np.float32) * np.float32(2.0) / np.float32(HEAD)
    ).astype(np.float32)
    table = jnp.asarray(np.concatenate([inverse_freq, inverse_freq])[None, :])
    hbm = pl.BlockSpec(memory_space=pl.ANY)
    vmem = pl.BlockSpec(memory_space=pltpu.VMEM)
    bf16, f32 = jnp.bfloat16, jnp.float32
    dma = pltpu.SemaphoreType.DMA
    return pl.pallas_call(
        kernel,
        out_shape=jax.ShapeDtypeStruct((TOK, 512), bf16),
        in_specs=[hbm] * 5 + [vmem],
        out_specs=vmem,
        scratch_shapes=[
            pltpu.VMEM((8, TOK, 512), bf16),
            pltpu.VMEM((NZ, NY, 2, 64, 768), bf16),
            pltpu.VMEM((NZ, NY, 2, 2, TOK, HEAD), bf16),
            pltpu.VMEM((NZ, NY, 2, 64, 512), bf16),
            pltpu.VMEM((512, 64), bf16),
            pltpu.VMEM((HEADS * TOK, HEAD), bf16),
            pltpu.VMEM((TOK, 768), f32),
            pltpu.VMEM((HEADS * TOK, HEAD), f32),
            pltpu.VMEM((HEADS * TOK, HEAD), f32),
            pltpu.VMEM((HEADS * TOK, HEAD), f32),
            pltpu.VMEM((TOK, 512), bf16),
            pltpu.VMEM((2, 4, TOK, 512), bf16),
            pltpu.VMEM((2, 3, TOK, 512), bf16),
            pltpu.VMEM((TOK, 512), bf16),
            pltpu.VMEM((TOK, 512), bf16),
            dma((5,)),
            dma((3, 2, 4, 4)),
            dma((3, 3)),
            dma((3, NZ)),
            dma((3, NZ, NY)),
            dma((3, NZ)),
            dma((7,)),
            dma((8,)),
            dma((2, 3)),
            dma((2, 3)),
            dma((1,)),
            dma((1,)),
        ],
        compiler_params=pltpu.CompilerParams(
            collective_id=0, has_side_effects=True, vmem_limit_bytes=50 * 2**20
        ),
    )(tokens, w_query, key_matrix, value_matrix, w_out, table)


def solution(mesh):
    in_specs = (
        P("ctx", "fsdp"),
        P("ctx", "fsdp"),
        P("ctx", "fsdp"),
        P("ctx", "fsdp"),
        P("fsdp", "ctx"),
    )
    out_specs = P("ctx", "fsdp")
    return jax.shard_map(body, mesh=mesh, in_specs=in_specs, out_specs=out_specs, check_vma=False)
```

time: 921 us -> 130 us (0.14); the launches traced: 912 us -> 130 us
  waiting for transfers between devices: 738 us -> 0 us
  matrix products: 144 us -> 0 us
  Pallas kernels: 0 us -> 126 us
  between operations: 13.6 us -> 0.04 us
  other arithmetic: 10.8 us -> 0 us
    all_gather x7 -> x0, waiting for transfers between devices: 647 us -> none  [the longest x1 120 us: body(): key_sum = add_rows(lax.all_gather(key_matrix, 'ctx', axis=0, tiled=True))]
    dot_general x132 -> x0, matrix products: 144 us -> none  [the longest x64 68.1 us: update(): jnp.einsum('gqk,kgd->gqd', exp_weights.astype(jnp.bfloat16), value_heads,...]
    pallas_call x0 -> x1, Pallas kernels: none -> 126 us  [body(): pl.pallas_call(kernel, out_shape=jax.ShapeDtypeStruct((TOK, 512), bf16),...]
    reduce_scatter x1 -> x0, waiting for transfers between devices: 88.1 us -> none  [body(): lax.psum_scatter(partial_out.astype(jnp.bfloat16), 'fsdp', scatter_dimens...]
  transfers between devices with their start and end apart: 8 -> 0, of which waited for: 7 -> 0; matrix products, arithmetic and copies ran while one was open for 16% -> 0% of each run, Pallas kernels for 0% -> 0%
where the time goes in v1:
time: 130 us
  Pallas kernels  126 us (97%)
  local copies, waits for them, and re-layouts  3.74 us (3%)
    pallas_call x1, Pallas kernels, body(): pl.pallas_call(kernel, out_shape=jax.ShapeDtypeStruct((TOK, 512), bf16),...  126 us
    unnamed x12, local copies, waits for them, and re-layouts  3.74 us

profile of v1, /device:TPU:1, one launch (start us, length us, event | category | flops | bytes accessed | tf_op | source)
XLA Modules:
  0.0 129.8 jit_solution(16924398872061531874)
XLA Ops:
  0.0 0.0 copy-start.1
  0.0 0.0 copy-start
  0.0 1.0 copy.7.wo
  1.0 0.0 copy-done.1
  1.0 0.0 copy-done
  1.0 0.0 copy-start.2
  1.0 0.7 copy-done.2
  1.7 0.0 copy-start.3
  1.7 0.7 copy-done.3
  2.5 0.0 copy-start.4
  2.5 0.7 copy-done.4
  3.1 126.1 %shard_map.64 = bf16[128,512]{1,0:T(8,128)(2,1)S(1)} custom-call(bf16[128,512]{1,0:T(8,128)(2,1)S(1)} %copy-done, bf16[64,512]{1,0:T(8,128)(2,1)S(1)} %copy-done.1, bf16[64,128]{1,0:T(8,128)(2,1)S(1)} %copy-done.2, bf16[64,128]{1,0:T(8,128)(2,1)S(1)} %copy-done.3, bf16[512,64]{1,0:T(8,128)(2,1)S(1)} %copy.7.wo, f32[1,128]{1,0:T(1,128)S(1)} %copy-done.4), custom_call_target="tpu_custom_call" | custom-call | tf_op jit(solution)/shard_map/pallas_call | solution.py:345
  129.2 0.7 copy.9
Async XLA Ops:
  0.0 1.0 copy-start.1
  0.0 1.0 copy-start
  1.0 0.7 copy-start.2
  1.7 0.7 copy-start.3
  2.5 0.7 copy-start.4

commit v2 on v1

v2 whole, which is shorter than its diff:
```python
import functools
import math

import jax
import jax.numpy as jnp
import numpy as np
from jax import lax
from jax.experimental import pallas as pl
from jax.experimental.pallas import tpu as pltpu
from jax.sharding import PartitionSpec as P

MESH = pl.DeviceIdType.MESH
HEAD = 128
HEADS = 4
NZ, NY = 8, 4
TOK = 128
SCALE2 = math.log2(math.e) / math.sqrt(HEAD)
REACH = ((4, 4, 3, 3), (3, 3, 4, 4))
WKV, WQ, KV, WO = 0, 1, 2, 3
COLUMNS = (4, 4, 4, 1)


def kernel(
    tok, wq, wk, wv, wo, invf, out,
    xbuf, wkvbuf, wqbuf, kvbuf, wobuf, table, qbuf, proj, mbuf, lbuf, acc, abuf, pbuf, rbuf, sbuf, ybuf,
    local, zsend, ysend, bsend, zrecv, brecv, tsend, trecv, asend, arecv, rsend, rrecv, hsend, hrecv,
):
    c = lax.axis_index("ctx")
    f = lax.axis_index("fsdp")
    k = c % 2
    y = (c // 2) % NY
    z = c // (2 * NY)
    x = f % 4
    yh = f // 4

    def at(zz, yy, kk):
        return ((zz * NY + yy) * 2 + kk, f)

    def up(d, n):
        return (z + (n if d == 0 else NZ - n)) % NZ

    near = (y, y + 1 - 2 * (y % 2), 2 - y // 2, 3 - 3 * (y // 2))
    bufs = (wkvbuf, wqbuf, kvbuf)

    def shard(g, zz, yy):
        return wobuf.at[zz, k] if g == WO else bufs[g].at[zz, yy, k]

    def zcopy(g, d, step, n):
        zz, yy = up(1 - d, step), near[n]
        ref = shard(g, zz, yy)
        return pltpu.make_async_remote_copy(
            src_ref=ref, dst_ref=ref, send_sem=zsend.at[g, d, step, n], recv_sem=zrecv.at[g, zz, yy],
            device_id=at(up(d, 1), y, k), device_id_type=MESH,
        )

    def ycopy(g, n):
        ref = shard(g, z, y)
        return pltpu.make_async_remote_copy(
            src_ref=ref, dst_ref=ref, send_sem=ysend.at[g, n - 1], recv_sem=zrecv.at[g, z, y],
            device_id=at(z, near[n], k), device_id_type=MESH,
        )

    def bcopy(g, zz, kk):
        ref = wobuf.at[:, kk] if g == WO else bufs[g].at[zz, :, kk]
        return pltpu.make_async_remote_copy(
            src_ref=ref, dst_ref=ref, send_sem=bsend.at[g, zz], recv_sem=brecv.at[g, zz],
            device_id=at(z, y, 1 - k), device_id_type=MESH,
        )

    def arrived(g, zz, yy):
        ref = shard(g, zz, yy)
        pltpu.make_async_remote_copy(
            src_ref=ref, dst_ref=ref, send_sem=zsend.at[g, 0, 0, 0], recv_sem=zrecv.at[g, zz, yy],
            device_id=at(z, y, 1 - k), device_id_type=MESH,
        ).wait_recv()

    def paired(g, zz):
        bcopy(g, zz, 1 - k).wait_recv()

    def open_y(g):
        for n in (1, 2, 3):
            ycopy(g, n).start()

    def open_z(g):
        for d in (0, 1):
            zcopy(g, d, 0, 0).start()

    def step0(g):
        for n in (1, 2, 3):
            arrived(g, z, near[n])
            for d in (0, 1):
                zcopy(g, d, 0, n).start()
        bcopy(g, z, k).start()

    def step(g, s):
        for n in range(COLUMNS[g]):
            for d in (0, 1):
                if s <= REACH[d][n]:
                    arrived(g, up(1 - d, s), near[n])
                    if s < REACH[d][n]:
                        zcopy(g, d, s, n).start()
        if g != WO:
            bcopy(g, up(1, s), k).start()
            if s < 4:
                bcopy(g, up(0, s), k).start()
        elif s == 4:
            bcopy(g, 0, k).start()

    def drain(g):
        for d in (0, 1):
            for n in range(COLUMNS[g]):
                for s in range(REACH[d][n]):
                    zcopy(g, d, s, n).wait_send()
        if g == WO:
            bcopy(g, 0, k).wait_send()
            return
        for n in (1, 2, 3):
            ycopy(g, n).wait_send()
        for s in range(NZ):
            bcopy(g, up(0, s), k).wait_send()

    def tcopy(n, slot, peer):
        ref = xbuf.at[slot]
        return pltpu.make_async_remote_copy(
            src_ref=ref, dst_ref=ref, send_sem=tsend.at[n], recv_sem=trecv.at[slot],
            device_id=(c, peer), device_id_type=MESH,
        )

    def tok_arrived(slot):
        tcopy(0, slot, yh * 4 + (x + 1) % 4).wait_recv()

    other = 1 - yh
    xr = yh * 4 + (x + 1) % 4
    xl = yh * 4 + (x + 3) % 4
    twin = other * 4 + x
    twin_l = other * 4 + (x + 3) % 4
    twin_r = other * 4 + (x + 1) % 4
    tokens_out = (
        (0, f, twin), (1, f, xr), (2, f, xl),
        (3, xl, xr),
        (4, twin, xr), (5, twin, xl),
        (6, twin_r, xl),
    )

    mine = wkvbuf.at[z, y, k]
    copies = [
        pltpu.make_async_copy(wk, mine.at[:, pl.ds(0, HEAD)], local.at[0]),
        pltpu.make_async_copy(wv, mine.at[:, pl.ds(HEAD, HEAD)], local.at[1]),
        pltpu.make_async_copy(wo, wobuf.at[z, k], local.at[2]),
        pltpu.make_async_copy(wq, wqbuf.at[z, y, k], local.at[3]),
        pltpu.make_async_copy(tok, xbuf.at[f], local.at[4]),
        pltpu.make_async_copy(invf, table, local.at[5]),
    ]
    for copy in copies:
        copy.start()

    barrier = pltpu.get_barrier_semaphore()
    peers = [at(up(0, 1), y, k), at(up(1, 1), y, k), at(z, y, 1 - k)]
    peers += [at(z, near[n], k) for n in (1, 2, 3)]
    peers += [(c, yh * 4 + (x + dx) % 4) for dx in (1, 2, 3)]
    peers += [((z * NY + near[n]) * 2 + k, twin) for n in (0, 1, 2, 3)]
    for peer in peers:
        pl.semaphore_signal(barrier, inc=1, device_id=peer, device_id_type=MESH)
    for copy in copies:
        copy.wait()
    pl.semaphore_wait(barrier, len(peers))

    open_z(WKV)
    open_y(WKV)
    open_z(WO)
    open_y(WQ)
    tcopy(*tokens_out[1]).start()
    tcopy(*tokens_out[2]).start()
    step0(WKV)
    open_z(WQ)
    step(WKV, 1)
    step(WO, 1)
    step0(WQ)
    tcopy(*tokens_out[0]).start()
    step(WKV, 2)
    step(WO, 2)
    tok_arrived(xl)
    tcopy(*tokens_out[3]).start()
    tok_arrived(xr)
    step(WKV, 3)
    step(WO, 3)
    step(WQ, 1)
    step(WKV, 4)
    step(WO, 4)

    position = (c * TOK + lax.broadcasted_iota(jnp.int32, (TOK, HEAD), 0)).astype(jnp.float32)
    angle = position * table[...]
    cosine = jnp.cos(angle)
    lane = lax.broadcasted_iota(jnp.int32, (TOK, HEAD), 1)
    sine = jnp.sin(angle) * jnp.where(lane < HEAD // 2, -1.0, 1.0).astype(jnp.float32)

    def turned(piece):
        return (piece * cosine + pltpu.roll(piece, HEAD // 2, 1) * sine).astype(jnp.bfloat16)

    tok_arrived(twin)
    tcopy(*tokens_out[4]).start()
    tcopy(*tokens_out[5]).start()
    step(WQ, 2)
    tok_arrived(twin_r)
    tcopy(*tokens_out[6]).start()
    tok_arrived(twin_l)
    tok_arrived(yh * 4 + (x + 2) % 4)
    tok_arrived(other * 4 + (x + 2) % 4)

    for s in range(NZ):
        paired(WKV, up(0, s))
    both = jnp.zeros((TOK, 2 * HEAD), jnp.float32)
    for s in range(NZ):
        both += jnp.dot(xbuf[s], wkvbuf[s].reshape(512, 2 * HEAD), preferred_element_type=jnp.float32)
    kvbuf[z, y, k, 0] = turned(both[:, :HEAD])
    kvbuf[z, y, k, 1] = both[:, HEAD:].astype(jnp.bfloat16)
    open_z(KV)
    open_y(KV)

    def multiply(zz, first=False):
        paired(WQ, zz)
        term = jnp.dot(xbuf[zz], wqbuf[zz].reshape(512, 512), preferred_element_type=jnp.float32)
        proj[...] = term if first else proj[...] + term

    step(WQ, 3)
    multiply(z, True)
    multiply(up(1, 1))
    multiply(up(0, 1))
    step0(KV)
    multiply(up(1, 2))
    multiply(up(0, 2))
    step(WQ, 4)
    step(KV, 1)
    multiply(up(1, 3))
    multiply(up(0, 3))
    multiply(up(0, 4))
    for h in range(HEADS):
        qbuf[pl.ds(h * TOK, TOK), :] = turned(proj[:, pl.ds(h * HEAD, HEAD)])

    rows = 256
    keys = NY * 2 * TOK

    def attend(zz, first=False):
        paired(KV, zz)

        def some():
            def body(i, carry):
                at_rows = pl.ds(pl.multiple_of(i * rows, rows), rows)
                key = kvbuf[zz, :, :, 0].reshape(keys, HEAD)
                value = kvbuf[zz, :, :, 1].reshape(keys, HEAD)
                score = lax.dot_general(
                    qbuf[at_rows, :], key, (((1,), (1,)), ((), ())), preferred_element_type=jnp.float32
                )
                if first:
                    key_at = lax.broadcasted_iota(jnp.int32, (rows, keys), 1)
                    query_at = (y * 2 + k) * TOK + lax.broadcasted_iota(jnp.int32, (rows, keys), 0) % TOK
                    score = jnp.where(key_at <= query_at, score, jnp.float32(-1e30))
                top = jnp.max(score, axis=1, keepdims=True)
                if first:
                    new = jnp.broadcast_to(top, (rows, HEAD))
                else:
                    old = mbuf[at_rows, :]
                    new = jnp.maximum(old, top)
                exps = jnp.exp2(score * SCALE2 - jnp.tile(new * SCALE2, (1, keys // HEAD)))
                total = jnp.sum(exps, axis=1, keepdims=True)
                summed = jnp.dot(exps.astype(jnp.bfloat16), value, preferred_element_type=jnp.float32)
                if first:
                    lbuf[at_rows, :] = jnp.broadcast_to(total, (rows, HEAD))
                    acc[at_rows, :] = summed
                else:
                    factor = jnp.exp2((old - new) * SCALE2)
                    lbuf[at_rows, :] = lbuf[at_rows, :] * factor + total
                    acc[at_rows, :] = acc[at_rows, :] * factor + summed
                mbuf[at_rows, :] = new
                return carry

            lax.fori_loop(0, HEADS * TOK // rows, body, 0)

        if first:
            some()
        else:
            pl.when(zz <= z)(some)

    attend(z, True)
    step(KV, 2)
    attend(up(1, 1))
    attend(up(0, 1))
    step(KV, 3)
    attend(up(1, 2))
    attend(up(0, 2))
    step(KV, 4)
    attend(up(1, 3))
    attend(up(0, 3))
    attend(up(0, 4))
    for h in range(HEADS):
        at_rows = pl.ds(h * TOK, TOK)
        abuf[y, :, pl.ds(h * HEAD, HEAD)] = (acc[at_rows, :] / lbuf[at_rows, :]).astype(jnp.bfloat16)

    def acopy(n, yy):
        ref = abuf.at[yy]
        return pltpu.make_async_remote_copy(
            src_ref=ref, dst_ref=ref, send_sem=asend.at[n - 1], recv_sem=arecv.at[yy],
            device_id=at(z, near[n], k), device_id_type=MESH,
        )

    for n in (1, 2, 3):
        acopy(n, y).start()
    bcopy(WO, 0, 1 - k).wait_recv()

    def rcopy(n, dx):
        there = (x + dx) % 4
        return pltpu.make_async_remote_copy(
            src_ref=pbuf.at[n, :, there], dst_ref=rbuf.at[n, dx - 1], send_sem=rsend.at[n, dx - 1],
            recv_sem=rrecv.at[n, dx - 1], device_id=(c, yh * 4 + there), device_id_type=MESH,
        )

    def make_terms(n):
        if n:
            acopy(n, near[n]).wait_recv()
        terms = lax.dot_general(
            abuf[near[n]], wobuf[...].reshape(1024, 512), (((1,), (1,)), ((), ())),
            preferred_element_type=jnp.float32,
        ).astype(jnp.bfloat16)
        for slot in range(8):
            pbuf[n, slot // 4, slot % 4] = terms[:, slot * HEAD:(slot + 1) * HEAD]
        for dx in (2, 1, 3):
            rcopy(n, dx).start()

    def hcopy(n, j):
        half = (other, yh)[j]
        return pltpu.make_async_remote_copy(
            src_ref=sbuf.at[n, j], dst_ref=ybuf.at[yh, y], send_sem=hsend.at[n, j], recv_sem=hrecv.at[yh, y],
            device_id=((z * NY + near[n]) * 2 + k, half * 4 + x), device_id_type=MESH,
        )

    def sum_over_x(n):
        for dx in (1, 3, 2):
            rcopy(n, dx).wait_recv()
        for j, half in ((0, other), (1, yh)):
            total = pbuf[n, half, x].astype(jnp.float32)
            for dx in (1, 2, 3):
                total = total + rbuf[n, dx - 1, half].astype(jnp.float32)
            if n == 0 and j == 1:
                ybuf[yh, y] = total.astype(jnp.bfloat16)
            else:
                sbuf[n, j] = total.astype(jnp.bfloat16)
                hcopy(n, j).start()

    make_terms(0)
    make_terms(1)
    sum_over_x(0)
    make_terms(2)
    sum_over_x(1)
    make_terms(3)
    sum_over_x(2)
    sum_over_x(3)
    for g in (WKV, WQ, KV, WO):
        drain(g)
    for entry in tokens_out:
        tcopy(*entry).wait_send()
    for n in (1, 2, 3):
        acopy(n, y).wait_send()
    for n in range(NY):
        for dx in (1, 2, 3):
            rcopy(n, dx).wait_send()
        for j in (0, 1):
            if n or j == 0:
                hcopy(n, j).wait_send()
                ref = ybuf.at[(other, yh)[j], near[n]]
                pltpu.make_async_remote_copy(
                    src_ref=ref, dst_ref=ref, send_sem=hsend.at[n, j],
                    recv_sem=hrecv.at[(other, yh)[j], near[n]],
                    device_id=(c, twin), device_id_type=MESH,
                ).wait_recv()
    for n in range(NY):
        out[:, pl.ds(n * HEAD, HEAD)] = (
            ybuf[0, n].astype(jnp.float32) + ybuf[1, n].astype(jnp.float32)
        ).astype(jnp.bfloat16)


def body(tokens, w_query, key_matrix, value_matrix, w_out):
    half = HEAD // 2
    inverse_freq = np.power(
        np.float32(500000.0), -np.arange(half, dtype=np.float32) * np.float32(2.0) / np.float32(HEAD)
    ).astype(np.float32)
    table = jnp.asarray(np.concatenate([inverse_freq, inverse_freq])[None, :])
    hbm = pl.BlockSpec(memory_space=pltpu.HBM)
    vmem = pl.BlockSpec(memory_space=pltpu.VMEM)
    bf16, f32 = jnp.bfloat16, jnp.float32
    dma = pltpu.SemaphoreType.DMA
    return pl.pallas_call(
        kernel,
        out_shape=jax.ShapeDtypeStruct((TOK, 512), bf16),
        in_specs=[hbm] * 6,
        out_specs=vmem,
        scratch_shapes=[
            pltpu.VMEM((8, TOK, 512), bf16),
            pltpu.VMEM((NZ, NY, 2, 64, 2 * HEAD), bf16),
            pltpu.VMEM((NZ, NY, 2, 64, 512), bf16),
            pltpu.VMEM((NZ, NY, 2, 2, TOK, HEAD), bf16),
            pltpu.VMEM((NZ, 2, 64, 512), bf16),
            pltpu.VMEM((1, HEAD), f32),
            pltpu.VMEM((HEADS * TOK, HEAD), bf16),
            pltpu.VMEM((TOK, 512), f32),
            pltpu.VMEM((HEADS * TOK, HEAD), f32),
            pltpu.VMEM((HEADS * TOK, HEAD), f32),
            pltpu.VMEM((HEADS * TOK, HEAD), f32),
            pltpu.VMEM((NY, TOK, 512), bf16),
            pltpu.VMEM((NY, 2, 4, TOK, HEAD), bf16),
            pltpu.VMEM((NY, 3, 2, TOK, HEAD), bf16),
            pltpu.VMEM((NY, 2, TOK, HEAD), bf16),
            pltpu.VMEM((2, NY, TOK, HEAD), bf16),
            dma((6,)),
            dma((4, 2, 4, 4)),
            dma((3, 3)),
            dma((4, NZ)),
            dma((4, NZ, NY)),
            dma((4, NZ)),
            dma((7,)),
            dma((8,)),
            dma((3,)),
            dma((NY,)),
            dma((NY, 3)),
            dma((NY, 3)),
            dma((NY, 2)),
            dma((2, NY)),
        ],
        compiler_params=pltpu.CompilerParams(
            collective_id=0, has_side_effects=True
        ),
    )(tokens, w_query, key_matrix, value_matrix, w_out.T, table)


def solution(mesh):
    in_specs = (
        P("ctx", "fsdp"),
        P("ctx", "fsdp"),
        P("ctx", "fsdp"),
        P("ctx", "fsdp"),
        P("fsdp", "ctx"),
    )
    out_specs = P("ctx", "fsdp")
    return jax.shard_map(body, mesh=mesh, in_specs=in_specs, out_specs=out_specs, check_vma=False)
```

time: 130 us -> 109 us (0.84)
  Pallas kernels: 126 us -> 107 us
  local copies, waits for them, and re-layouts: 3.74 us -> 1.57 us
    pallas_call x1, Pallas kernels: 126 us -> 107 us  [body(): pl.pallas_call(kernel, out_shape=jax.ShapeDtypeStruct((TOK, 512), bf16),...]
    unnamed x12 -> x1, local copies, waits for them, and re-layouts: 3.74 us -> 1.57 us
where the time goes in v2:
time: 109 us
  Pallas kernels  107 us (98%)
  local copies, waits for them, and re-layouts  1.57 us (1%)
    pallas_call x1, Pallas kernels, body(): pl.pallas_call(kernel, out_shape=jax.ShapeDtypeStruct((TOK, 512), bf16),...  107 us

profile of v2, /device:TPU:1, one launch (start us, length us, event | category | flops | bytes accessed | tf_op | source)
XLA Modules:
  0.0 108.7 jit_solution(5731267511834953715)
XLA Ops:
  0.0 107.1 %shard_map.64 = bf16[128,512]{1,0:T(8,128)(2,1)} custom-call(bf16[128,512]{1,0:T(8,128)(2,1)} %tok.1, bf16[64,512]{1,0:T(8,128)(2,1)} %wq.1, bf16[64,128]{1,0:T(8,128)(2,1)} %wk.1, bf16[64,128]{1,0:T(8,128)(2,1)} %wv.1, bf16[64,512]{1,0:T(8,128)(2,1)} %bitcast.1, f32[1,128]{1,0:T(1,128)} %constant.2.clone.invf), custom_call_target="tpu_custom_call" | custom-call | tf_op jit(solution)/shard_map/pallas_call | solution.py:391
  107.1 1.6 %copy.8 = bf16[128,512]{1,0:T(8,128)(2,1)} copy(bf16[128,512]{1,0:T(8,128)(2,1)} %shard_map.64) | data formatting | bytes 262144

commit v3 on v2

--- a/solution.py
+++ b/solution.py
@@ -15,15 +15,15 @@
 NZ, NY = 8, 4
 TOK = 128
 SCALE2 = math.log2(math.e) / math.sqrt(HEAD)
-REACH = ((4, 4, 3, 3), (3, 3, 4, 4))
-WKV, WQ, KV, WO = 0, 1, 2, 3
-COLUMNS = (4, 4, 4, 1)
+REACH = ((4, 3), (3, 4))
+WKV, WQ, KV, WO, WB = 0, 1, 2, 3, 4
+FIRST = 48
 
 
 def kernel(
     tok, wq, wk, wv, wo, invf, out,
     xbuf, wkvbuf, wqbuf, kvbuf, wobuf, table, qbuf, proj, mbuf, lbuf, acc, abuf, pbuf, rbuf, sbuf, ybuf,
-    local, zsend, ysend, bsend, zrecv, brecv, tsend, trecv, asend, arecv, rsend, rrecv, hsend, hrecv,
+    local, zsend, ysend, bsend, zrecv, yrecv, brecv, orecv, tsend, trecv, lsend, lrecv, asend, arecv, rsend, rrecv, hsend, hrecv,
 ):
     c = lax.axis_index("ctx")
     f = lax.axis_index("fsdp")
@@ -42,37 +42,46 @@
     near = (y, y + 1 - 2 * (y % 2), 2 - y // 2, 3 - 3 * (y // 2))
     bufs = (wkvbuf, wqbuf, kvbuf)
 
-    def shard(g, zz, yy):
-        return wobuf.at[zz, k] if g == WO else bufs[g].at[zz, yy, k]
-
-    def zcopy(g, d, step, n):
-        zz, yy = up(1 - d, step), near[n]
-        ref = shard(g, zz, yy)
+    base = (2 * (y // 2), 2 - 2 * (y // 2))
+
+    def remote(ref, send, recv, peer):
         return pltpu.make_async_remote_copy(
-            src_ref=ref, dst_ref=ref, send_sem=zsend.at[g, d, step, n], recv_sem=zrecv.at[g, zz, yy],
-            device_id=at(up(d, 1), y, k), device_id_type=MESH,
+            src_ref=ref, dst_ref=ref, send_sem=send, recv_sem=recv, device_id=peer, device_id_type=MESH
         )
 
+    def view(g, zz, yy, kk):
+        if g == WQ:
+            return wqbuf.at[zz, yy, kk, pl.ds(0, FIRST)]
+        return bufs[g].at[zz, yy, kk]
+
+    def late(zz, yy, kk):
+        return wqbuf.at[zz, yy, kk, pl.ds(FIRST, 64 - FIRST)]
+
+    def pair(g, zz, p):
+        if g == WO:
+            return wobuf.at[zz, k]
+        if g == WB:
+            return late(zz, y, k)
+        return view(g, zz, pl.ds(base[p], 2), k)
+
+    def recv_of(g, zz, p):
+        return orecv.at[g - WO, zz] if g >= WO else zrecv.at[g, zz, p]
+
+    def zcopy(g, d, step, p):
+        zz = up(1 - d, step)
+        return remote(pair(g, zz, p), zsend.at[g], recv_of(g, zz, p), at(up(d, 1), y, k))
+
+    def zfirst(g, d, n):
+        return remote(view(g, z, near[n], k), zsend.at[g], zrecv.at[g, z, 0], at(up(d, 1), y, k))
+
     def ycopy(g, n):
-        ref = shard(g, z, y)
-        return pltpu.make_async_remote_copy(
-            src_ref=ref, dst_ref=ref, send_sem=ysend.at[g, n - 1], recv_sem=zrecv.at[g, z, y],
-            device_id=at(z, near[n], k), device_id_type=MESH,
-        )
+        return remote(view(g, z, y, k), ysend.at[g], yrecv.at[g, min(n, 2) - 1], at(z, near[n], k))
+
+    sibling = at(z, y, 1 - k)
 
     def bcopy(g, zz, kk):
-        ref = wobuf.at[:, kk] if g == WO else bufs[g].at[zz, :, kk]
-        return pltpu.make_async_remote_copy(
-            src_ref=ref, dst_ref=ref, send_sem=bsend.at[g, zz], recv_sem=brecv.at[g, zz],
-            device_id=at(z, y, 1 - k), device_id_type=MESH,
-        )
-
-    def arrived(g, zz, yy):
-        ref = shard(g, zz, yy)
-        pltpu.make_async_remote_copy(
-            src_ref=ref, dst_ref=ref, send_sem=zsend.at[g, 0, 0, 0], recv_sem=zrecv.at[g, zz, yy],
-            device_id=at(z, y, 1 - k), device_id_type=MESH,
-        ).wait_recv()
+        ref = wobuf.at[:, kk] if g == WO else late(slice(None), slice(None), kk) if g == WB else view(g, zz, slice(None), kk)
+        return remote(ref, bsend.at[g], brecv.at[g, zz], sibling)
 
     def paired(g, zz):
         bcopy(g, zz, 1 - k).wait_recv()
@@ -83,51 +92,59 @@
 
     def open_z(g):
         for d in (0, 1):
-            zcopy(g, d, 0, 0).start()
-
-    def step0(g):
-        for n in (1, 2, 3):
-            arrived(g, z, near[n])
+            if g >= WO:
+                zcopy(g, d, 0, 0).start()
+            else:
+                zfirst(g, d, 0).start()
+
+    def step0a(g):
+        remote(view(g, z, near[1], k), ysend.at[g], yrecv.at[g, 0], sibling).wait_recv()
+        for d in (0, 1):
+            zfirst(g, d, 1).start()
+
+    def step0b(g):
+        remote(pair(g, z, 1), ysend.at[g], yrecv.at[g, 1], sibling).wait_recv()
+        for d in (0, 1):
+            zcopy(g, d, 0, 1).start()
+        bcopy(g, z, k).start()
+
+    def step(g, s):
+        for p in (0, 1):
             for d in (0, 1):
-                zcopy(g, d, 0, n).start()
-        bcopy(g, z, k).start()
-
-    def step(g, s):
-        for n in range(COLUMNS[g]):
-            for d in (0, 1):
-                if s <= REACH[d][n]:
-                    arrived(g, up(1 - d, s), near[n])
-                    if s < REACH[d][n]:
-                        zcopy(g, d, s, n).start()
-        if g != WO:
+                if s <= REACH[d][p] and (g < WO or p == 0):
+                    zz = up(1 - d, s)
+                    remote(pair(g, zz, p), zsend.at[g], recv_of(g, zz, p), sibling).wait_recv()
+                    if s < REACH[d][p]:
+                        zcopy(g, d, s, p).start()
+        if g < WO:
             bcopy(g, up(1, s), k).start()
             if s < 4:
                 bcopy(g, up(0, s), k).start()
-        elif s == 4:
+        elif s == 4 and g == WO:
             bcopy(g, 0, k).start()
 
+    def wcopy(n, yy):
+        return remote(late(slice(None), yy, k), lsend.at[0], lrecv.at[yy], at(z, near[n], k))
+
     def drain(g):
-        for d in (0, 1):
-            for n in range(COLUMNS[g]):
-                for s in range(REACH[d][n]):
-                    zcopy(g, d, s, n).wait_send()
         if g == WO:
+            remote(wobuf.at[pl.ds(0, 7), k], zsend.at[g], orecv.at[0, 0], sibling).wait_send()
             bcopy(g, 0, k).wait_send()
             return
-        for n in (1, 2, 3):
-            ycopy(g, n).wait_send()
-        for s in range(NZ):
-            bcopy(g, up(0, s), k).wait_send()
-
-    def tcopy(n, slot, peer):
-        ref = xbuf.at[slot]
-        return pltpu.make_async_remote_copy(
-            src_ref=ref, dst_ref=ref, send_sem=tsend.at[n], recv_sem=trecv.at[slot],
-            device_id=(c, peer), device_id_type=MESH,
-        )
+        if g == WB:
+            remote(late(pl.ds(0, 7), y, k), zsend.at[g], orecv.at[0, 0], sibling).wait_send()
+            remote(late(slice(None), pl.ds(0, 3), k), lsend.at[0], orecv.at[0, 0], sibling).wait_send()
+            bcopy(g, 0, k).wait_send()
+            return
+        remote(view(g, pl.ds(0, 7), slice(None), k), zsend.at[g], orecv.at[0, 0], sibling).wait_send()
+        remote(view(g, 0, pl.ds(0, 3), k), ysend.at[g], orecv.at[0, 0], sibling).wait_send()
+        remote(view(g, slice(None), slice(None), k), bsend.at[g], orecv.at[0, 0], sibling).wait_send()
+
+    def tcopy(slot, peer):
+        return remote(xbuf.at[slot], tsend.at[0], trecv.at[slot], (c, peer))
 
     def tok_arrived(slot):
-        tcopy(0, slot, yh * 4 + (x + 1) % 4).wait_recv()
+        tcopy(slot, yh * 4 + (x + 1) % 4).wait_recv()
 
     other = 1 - yh
     xr = yh * 4 + (x + 1) % 4
@@ -136,10 +153,10 @@
     twin_l = other * 4 + (x + 3) % 4
     twin_r = other * 4 + (x + 1) % 4
     tokens_out = (
-        (0, f, twin), (1, f, xr), (2, f, xl),
-        (3, xl, xr),
-        (4, twin, xr), (5, twin, xl),
-        (6, twin_r, xl),
+        (f, twin), (f, xr), (f, xl),
+        (xl, xr),
+        (twin, xr), (twin, xl),
+        (twin_r, xl),
     )
 
     mine = wkvbuf.at[z, y, k]
@@ -167,26 +184,38 @@
 
     open_z(WKV)
     open_y(WKV)
+    open_z(WB)
     open_z(WO)
+    open_z(WQ)
     open_y(WQ)
     tcopy(*tokens_out[1]).start()
     tcopy(*tokens_out[2]).start()
-    step0(WKV)
-    open_z(WQ)
+    step0a(WKV)
+    step(WB, 1)
+    step(WO, 1)
+    step0a(WQ)
+    step0b(WKV)
+    step(WB, 2)
     step(WKV, 1)
-    step(WO, 1)
-    step0(WQ)
+    step(WO, 2)
+    step0b(WQ)
     tcopy(*tokens_out[0]).start()
+    step(WB, 3)
     step(WKV, 2)
-    step(WO, 2)
+    step(WO, 3)
     tok_arrived(xl)
     tcopy(*tokens_out[3]).start()
     tok_arrived(xr)
+    step(WB, 4)
+    for n in (1, 2, 3):
+        wcopy(n, y).start()
     step(WKV, 3)
-    step(WO, 3)
+    step(WO, 4)
     step(WQ, 1)
+    tok_arrived(twin)
+    tcopy(*tokens_out[4]).start()
+    tcopy(*tokens_out[5]).start()
     step(WKV, 4)
-    step(WO, 4)
 
     position = (c * TOK + lax.broadcasted_iota(jnp.int32, (TOK, HEAD), 0)).astype(jnp.float32)
     angle = position * table[...]
@@ -197,12 +226,9 @@
     def turned(piece):
         return (piece * cosine + pltpu.roll(piece, HEAD // 2, 1) * sine).astype(jnp.bfloat16)
 
-    tok_arrived(twin)
-    tcopy(*tokens_out[4]).start()
-    tcopy(*tokens_out[5]).start()
-    step(WQ, 2)
     tok_arrived(twin_r)
     tcopy(*tokens_out[6]).start()
+    step(WQ, 2)
     tok_arrived(twin_l)
     tok_arrived(yh * 4 + (x + 2) % 4)
     tok_arrived(other * 4 + (x + 2) % 4)
@@ -223,10 +249,15 @@
         proj[...] = term if first else proj[...] + term
 
     step(WQ, 3)
+    for n in (1, 2, 3):
+        wcopy(n, near[n]).wait_recv()
+    bcopy(WB, 0, k).start()
+    step0a(KV)
+    step0b(KV)
+    bcopy(WB, 0, 1 - k).wait_recv()
     multiply(z, True)
     multiply(up(1, 1))
     multiply(up(0, 1))
-    step0(KV)
     multiply(up(1, 2))
     multiply(up(0, 2))
     step(WQ, 4)
@@ -281,42 +312,48 @@
         else:
             pl.when(zz <= z)(some)
 
+    inner = jnp.logical_or(y == 1, y == 2)
+
+    def acopy(kind, n, yy):
+        return remote(abuf.at[yy], asend.at[kind], arecv.at[yy], at(z, near[n], k))
+
+    def finish():
+        for h in range(HEADS):
+            at_rows = pl.ds(h * TOK, TOK)
+            abuf[y, :, pl.ds(h * HEAD, HEAD)] = (acc[at_rows, :] / lbuf[at_rows, :]).astype(jnp.bfloat16)
+        acopy(0, 1, y).start()
+        pl.when(inner)(lambda: acopy(1, 2, y).start())
+
     attend(z, True)
+    pl.when(z == 0)(finish)
     step(KV, 2)
     attend(up(1, 1))
     attend(up(0, 1))
+    pl.when(z == 1)(finish)
     step(KV, 3)
     attend(up(1, 2))
     attend(up(0, 2))
+    pl.when(z == 2)(finish)
     step(KV, 4)
     attend(up(1, 3))
     attend(up(0, 3))
     attend(up(0, 4))
-    for h in range(HEADS):
-        at_rows = pl.ds(h * TOK, TOK)
-        abuf[y, :, pl.ds(h * HEAD, HEAD)] = (acc[at_rows, :] / lbuf[at_rows, :]).astype(jnp.bfloat16)
-
-    def acopy(n, yy):
-        ref = abuf.at[yy]
-        return pltpu.make_async_remote_copy(
-            src_ref=ref, dst_ref=ref, send_sem=asend.at[n - 1], recv_sem=arecv.at[yy],
-            device_id=at(z, near[n], k), device_id_type=MESH,
-        )
-
-    for n in (1, 2, 3):
-        acopy(n, y).start()
+    pl.when(z >= 3)(finish)
+
     bcopy(WO, 0, 1 - k).wait_recv()
 
     def rcopy(n, dx):
         there = (x + dx) % 4
         return pltpu.make_async_remote_copy(
-            src_ref=pbuf.at[n, :, there], dst_ref=rbuf.at[n, dx - 1], send_sem=rsend.at[n, dx - 1],
-            recv_sem=rrecv.at[n, dx - 1], device_id=(c, yh * 4 + there), device_id_type=MESH,
+            src_ref=pbuf.at[n, :, there], dst_ref=rbuf.at[n, dx - 1], send_sem=rsend.at[0],
+            recv_sem=rrecv.at[n], device_id=(c, yh * 4 + there), device_id_type=MESH,
         )
 
+    def pass_on(n):
+        acopy(0, 1, near[n]).wait_recv()
+        pl.when(inner)(lambda: acopy(1 + n, 2 if n == 1 else 1, near[n]).start())
+
     def make_terms(n):
-        if n:
-            acopy(n, near[n]).wait_recv()
         terms = lax.dot_general(
             abuf[near[n]], wobuf[...].reshape(1024, 512), (((1,), (1,)), ((), ())),
             preferred_element_type=jnp.float32,
@@ -329,52 +366,49 @@
     def hcopy(n, j):
         half = (other, yh)[j]
         return pltpu.make_async_remote_copy(
-            src_ref=sbuf.at[n, j], dst_ref=ybuf.at[yh, y], send_sem=hsend.at[n, j], recv_sem=hrecv.at[yh, y],
+            src_ref=sbuf.at[n, j], dst_ref=ybuf.at[yh * 4 + y], send_sem=hsend.at[0], recv_sem=hrecv.at[0],
             device_id=((z * NY + near[n]) * 2 + k, half * 4 + x), device_id_type=MESH,
         )
 
     def sum_over_x(n):
-        for dx in (1, 3, 2):
-            rcopy(n, dx).wait_recv()
+        remote(rbuf.at[n], rsend.at[0], rrecv.at[n], sibling).wait_recv()
         for j, half in ((0, other), (1, yh)):
             total = pbuf[n, half, x].astype(jnp.float32)
             for dx in (1, 2, 3):
                 total = total + rbuf[n, dx - 1, half].astype(jnp.float32)
             if n == 0 and j == 1:
-                ybuf[yh, y] = total.astype(jnp.bfloat16)
+                ybuf[yh * 4 + y] = total.astype(jnp.bfloat16)
             else:
                 sbuf[n, j] = total.astype(jnp.bfloat16)
                 hcopy(n, j).start()
 
     make_terms(0)
+    pass_on(1)
     make_terms(1)
+    pass_on(2)
+    make_terms(2)
     sum_over_x(0)
-    make_terms(2)
+    pass_on(3)
+    make_terms(3)
     sum_over_x(1)
-    make_terms(3)
     sum_over_x(2)
     sum_over_x(3)
-    for g in (WKV, WQ, KV, WO):
+    for g in (WKV, WQ, KV, WO, WB):
         drain(g)
-    for entry in tokens_out:
-        tcopy(*entry).wait_send()
-    for n in (1, 2, 3):
-        acopy(n, y).wait_send()
-    for n in range(NY):
-        for dx in (1, 2, 3):
-            rcopy(n, dx).wait_send()
-        for j in (0, 1):
-            if n or j == 0:
-                hcopy(n, j).wait_send()
-                ref = ybuf.at[(other, yh)[j], near[n]]
-                pltpu.make_async_remote_copy(
-                    src_ref=ref, dst_ref=ref, send_sem=hsend.at[n, j],
-                    recv_sem=hrecv.at[(other, yh)[j], near[n]],
-                    device_id=(c, twin), device_id_type=MESH,
-                ).wait_recv()
+    remote(xbuf.at[pl.ds(0, 7)], tsend.at[0], orecv.at[0, 0], sibling).wait_send()
+    acopy(0, 1, y).wait_send()
+
+    @pl.when(inner)
+    def _():
+        for kind in (1, 2, 3, 4):
+            acopy(kind, 1, y).wait_send()
+
+    remote(rbuf, rsend.at[0], orecv.at[0, 0], sibling).wait_send()
+    remote(ybuf.at[pl.ds(0, 7)], hsend.at[0], hrecv.at[0], sibling).wait_send()
+    remote(ybuf.at[pl.ds(0, 7)], hsend.at[0], hrecv.at[0], sibling).wait_recv()
     for n in range(NY):
         out[:, pl.ds(n * HEAD, HEAD)] = (
-            ybuf[0, n].astype(jnp.float32) + ybuf[1, n].astype(jnp.float32)
+            ybuf[n].astype(jnp.float32) + ybuf[4 + n].astype(jnp.float32)
         ).astype(jnp.bfloat16)
 
 
@@ -409,21 +443,25 @@
             pltpu.VMEM((NY, 2, 4, TOK, HEAD), bf16),
             pltpu.VMEM((NY, 3, 2, TOK, HEAD), bf16),
             pltpu.VMEM((NY, 2, TOK, HEAD), bf16),
-            pltpu.VMEM((2, NY, TOK, HEAD), bf16),
+            pltpu.VMEM((2 * NY, TOK, HEAD), bf16),
             dma((6,)),
-            dma((4, 2, 4, 4)),
-            dma((3, 3)),
-            dma((4, NZ)),
-            dma((4, NZ, NY)),
-            dma((4, NZ)),
-            dma((7,)),
+            dma((5,)),
+            dma((3,)),
+            dma((5,)),
+            dma((3, NZ, 2)),
+            dma((3, 2)),
+            dma((5, NZ)),
+            dma((2, NZ)),
+            dma((1,)),
             dma((8,)),
-            dma((3,)),
+            dma((1,)),
             dma((NY,)),
-            dma((NY, 3)),
-            dma((NY, 3)),
-            dma((NY, 2)),
-            dma((2, NY)),
+            dma((5,)),
+            dma((NY,)),
+            dma((1,)),
+            dma((NY,)),
+            dma((1,)),
+            dma((1,)),
         ],
         compiler_params=pltpu.CompilerParams(
             collective_id=0, has_side_effects=True

time: 109 us -> 98.7 us (0.906)
  Pallas kernels: 107 us -> 96 us
    pallas_call x1, Pallas kernels: 107 us -> 96 us  [body(): pl.pallas_call(kernel, out_shape=jax.ShapeDtypeStruct((TOK, 512), bf16),...]
where the time goes in v3:
time: 98.7 us; the launch traced here: 97.6 us
  Pallas kernels  96 us (97%)
  local copies, waits for them, and re-layouts  1.57 us (2%)
    pallas_call x1, Pallas kernels, body(): pl.pallas_call(kernel, out_shape=jax.ShapeDtypeStruct((TOK, 512), bf16),...  96 us

profile of v3, /device:TPU:1, one launch (start us, length us, event | category | flops | bytes accessed | tf_op | source)
XLA Modules:
  0.0 97.6 jit_solution(6781585574438801419)
XLA Ops:
  0.0 96.0 %shard_map.64 = bf16[128,512]{1,0:T(8,128)(2,1)} custom-call(bf16[128,512]{1,0:T(8,128)(2,1)} %tok.1, bf16[64,512]{1,0:T(8,128)(2,1)} %wq.1, bf16[64,128]{1,0:T(8,128)(2,1)} %wk.1, bf16[64,128]{1,0:T(8,128)(2,1)} %wv.1, bf16[64,512]{1,0:T(8,128)(2,1)} %bitcast.1, f32[1,128]{1,0:T(1,128)} %constant.2.clone.invf), custom_call_target="tpu_custom_call" | custom-call | tf_op jit(solution)/shard_map/pallas_call | solution.py:425
  96.1 1.6 %copy.8 = bf16[128,512]{1,0:T(8,128)(2,1)} copy(bf16[128,512]{1,0:T(8,128)(2,1)} %shard_map.64) | data formatting | bytes 262144

commit v4 on v3

--- a/solution.py
+++ b/solution.py
@@ -14,6 +14,7 @@
 HEADS = 4
 NZ, NY = 8, 4
 TOK = 128
+HALF = TOK // 2
 SCALE2 = math.log2(math.e) / math.sqrt(HEAD)
 REACH = ((4, 3), (3, 4))
 WKV, WQ, KV, WO, WB = 0, 1, 2, 3, 4
@@ -97,26 +98,28 @@
             else:
                 zfirst(g, d, 0).start()
 
-    def step0a(g):
+    def step0a(g, last):
         remote(view(g, z, near[1], k), ysend.at[g], yrecv.at[g, 0], sibling).wait_recv()
         for d in (0, 1):
             zfirst(g, d, 1).start()
-
-    def step0b(g):
+        if last:
+            bcopy(g, z, k).start()
+
+    def step0b(g, last):
         remote(pair(g, z, 1), ysend.at[g], yrecv.at[g, 1], sibling).wait_recv()
         for d in (0, 1):
             zcopy(g, d, 0, 1).start()
-        bcopy(g, z, k).start()
-
-    def step(g, s):
-        for p in (0, 1):
-            for d in (0, 1):
-                if s <= REACH[d][p] and (g < WO or p == 0):
-                    zz = up(1 - d, s)
-                    remote(pair(g, zz, p), zsend.at[g], recv_of(g, zz, p), sibling).wait_recv()
-                    if s < REACH[d][p]:
-                        zcopy(g, d, s, p).start()
-        if g < WO:
+        if last:
+            bcopy(g, z, k).start()
+
+    def step(g, s, p, last):
+        for d in (0, 1):
+            if s <= REACH[d][p]:
+                zz = up(1 - d, s)
+                remote(pair(g, zz, p), zsend.at[g], recv_of(g, zz, p), sibling).wait_recv()
+                if s < REACH[d][p]:
+                    zcopy(g, d, s, p).start()
+        if g < WO and last:
             bcopy(g, up(1, s), k).start()
             if s < 4:
                 bcopy(g, up(0, s), k).start()
@@ -190,32 +193,6 @@
     open_y(WQ)
     tcopy(*tokens_out[1]).start()
     tcopy(*tokens_out[2]).start()
-    step0a(WKV)
-    step(WB, 1)
-    step(WO, 1)
-    step0a(WQ)
-    step0b(WKV)
-    step(WB, 2)
-    step(WKV, 1)
-    step(WO, 2)
-    step0b(WQ)
-    tcopy(*tokens_out[0]).start()
-    step(WB, 3)
-    step(WKV, 2)
-    step(WO, 3)
-    tok_arrived(xl)
-    tcopy(*tokens_out[3]).start()
-    tok_arrived(xr)
-    step(WB, 4)
-    for n in (1, 2, 3):
-        wcopy(n, y).start()
-    step(WKV, 3)
-    step(WO, 4)
-    step(WQ, 1)
-    tok_arrived(twin)
-    tcopy(*tokens_out[4]).start()
-    tcopy(*tokens_out[5]).start()
-    step(WKV, 4)
 
     position = (c * TOK + lax.broadcasted_iota(jnp.int32, (TOK, HEAD), 0)).astype(jnp.float32)
     angle = position * table[...]
@@ -226,47 +203,38 @@
     def turned(piece):
         return (piece * cosine + pltpu.roll(piece, HEAD // 2, 1) * sine).astype(jnp.bfloat16)
 
-    tok_arrived(twin_r)
-    tcopy(*tokens_out[6]).start()
-    step(WQ, 2)
-    tok_arrived(twin_l)
-    tok_arrived(yh * 4 + (x + 2) % 4)
-    tok_arrived(other * 4 + (x + 2) % 4)
-
-    for s in range(NZ):
-        paired(WKV, up(0, s))
-    both = jnp.zeros((TOK, 2 * HEAD), jnp.float32)
-    for s in range(NZ):
-        both += jnp.dot(xbuf[s], wkvbuf[s].reshape(512, 2 * HEAD), preferred_element_type=jnp.float32)
-    kvbuf[z, y, k, 0] = turned(both[:, :HEAD])
-    kvbuf[z, y, k, 1] = both[:, HEAD:].astype(jnp.bfloat16)
-    open_z(KV)
-    open_y(KV)
-
-    def multiply(zz, first=False):
-        paired(WQ, zz)
-        term = jnp.dot(xbuf[zz], wqbuf[zz].reshape(512, 512), preferred_element_type=jnp.float32)
-        proj[...] = term if first else proj[...] + term
-
-    step(WQ, 3)
-    for n in (1, 2, 3):
-        wcopy(n, near[n]).wait_recv()
-    bcopy(WB, 0, k).start()
-    step0a(KV)
-    step0b(KV)
-    bcopy(WB, 0, 1 - k).wait_recv()
-    multiply(z, True)
-    multiply(up(1, 1))
-    multiply(up(0, 1))
-    multiply(up(1, 2))
-    multiply(up(0, 2))
-    step(WQ, 4)
-    step(KV, 1)
-    multiply(up(1, 3))
-    multiply(up(0, 3))
-    multiply(up(0, 4))
-    for h in range(HEADS):
-        qbuf[pl.ds(h * TOK, TOK), :] = turned(proj[:, pl.ds(h * HEAD, HEAD)])
+    def send_late():
+        for n in (1, 2, 3):
+            wcopy(n, y).start()
+
+    def take_late():
+        for n in (1, 2, 3):
+            wcopy(n, near[n]).wait_recv()
+        bcopy(WB, 0, k).start()
+
+    def make_keys():
+        tok_arrived(twin_l)
+        tok_arrived(yh * 4 + (x + 2) % 4)
+        tok_arrived(other * 4 + (x + 2) % 4)
+        for s in range(NZ):
+            paired(WKV, up(0, s))
+        both = jnp.zeros((TOK, 2 * HEAD), jnp.float32)
+        for s in range(NZ):
+            both += jnp.dot(xbuf[s], wkvbuf[s].reshape(512, 2 * HEAD), preferred_element_type=jnp.float32)
+        kvbuf[z, y, k, 0] = turned(both[:, :HEAD])
+        kvbuf[z, y, k, 1] = both[:, HEAD:].astype(jnp.bfloat16)
+        open_z(KV)
+        open_y(KV)
+
+    def make_queries():
+        bcopy(WB, 0, 1 - k).wait_recv()
+        for n in range(NZ):
+            zz = up(n % 2, (n + 1) // 2)
+            paired(WQ, zz)
+            term = jnp.dot(xbuf[zz], wqbuf[zz].reshape(512, 512), preferred_element_type=jnp.float32)
+            proj[...] = term if n == 0 else proj[...] + term
+        for h in range(HEADS):
+            qbuf[pl.ds(h * TOK, TOK), :] = turned(proj[:, pl.ds(h * HEAD, HEAD)])
 
     rows = 256
     keys = NY * 2 * TOK
@@ -314,94 +282,161 @@
 
     inner = jnp.logical_or(y == 1, y == 2)
 
-    def acopy(kind, n, yy):
-        return remote(abuf.at[yy], asend.at[kind], arecv.at[yy], at(z, near[n], k))
+    def acopy(kind, n, yy, h):
+        ref = abuf.at[yy, pl.ds(h * HALF, HALF)]
+        return remote(ref, asend.at[kind], arecv.at[yy, h], at(z, near[n], k))
 
     def finish():
         for h in range(HEADS):
             at_rows = pl.ds(h * TOK, TOK)
             abuf[y, :, pl.ds(h * HEAD, HEAD)] = (acc[at_rows, :] / lbuf[at_rows, :]).astype(jnp.bfloat16)
-        acopy(0, 1, y).start()
-        pl.when(inner)(lambda: acopy(1, 2, y).start())
-
+        for h in (0, 1):
+            acopy(0, 1, y, h).start()
+
+            @pl.when(inner)
+            def _():
+                acopy(1, 2, y, h).start()
+
+    step0a(WKV, False)
+    step(WB, 1, 0, True)
+    step(WO, 1, 0, True)
+    step0a(WQ, False)
+    step0b(WKV, True)
+    step(WB, 2, 0, True)
+    step(WKV, 1, 0, False)
+    step(WKV, 1, 1, True)
+    step(WO, 2, 0, True)
+    step0b(WQ, True)
+    tcopy(*tokens_out[0]).start()
+    step(WB, 3, 0, True)
+    step(WKV, 2, 0, False)
+    step(WKV, 2, 1, True)
+    step(WO, 3, 0, True)
+    tok_arrived(xl)
+    tcopy(*tokens_out[3]).start()
+    tok_arrived(xr)
+    step(WB, 4, 0, True)
+    send_late()
+    step(WKV, 3, 0, False)
+    step(WKV, 3, 1, True)
+    step(WO, 4, 0, True)
+    step(WQ, 1, 0, False)
+    step(WQ, 1, 1, True)
+    tok_arrived(twin)
+    tcopy(*tokens_out[4]).start()
+    tcopy(*tokens_out[5]).start()
+    step(WKV, 4, 0, False)
+    step(WKV, 4, 1, True)
+    tok_arrived(twin_r)
+    tcopy(*tokens_out[6]).start()
+    step(WQ, 2, 0, False)
+    step(WQ, 2, 1, True)
+    make_keys()
+    step(WQ, 3, 0, False)
+    step(WQ, 3, 1, True)
+    take_late()
+    step0a(KV, False)
+    step0b(KV, True)
+    step(WQ, 4, 0, False)
+    step(WQ, 4, 1, True)
+    step(KV, 1, 0, False)
+    step(KV, 1, 1, True)
+    make_queries()
     attend(z, True)
     pl.when(z == 0)(finish)
-    step(KV, 2)
+    step(KV, 2, 0, False)
+    step(KV, 2, 1, True)
     attend(up(1, 1))
     attend(up(0, 1))
     pl.when(z == 1)(finish)
-    step(KV, 3)
+    step(KV, 3, 0, False)
+    step(KV, 3, 1, True)
     attend(up(1, 2))
     attend(up(0, 2))
     pl.when(z == 2)(finish)
-    step(KV, 4)
+    step(KV, 4, 0, False)
+    step(KV, 4, 1, True)
     attend(up(1, 3))
     attend(up(0, 3))
-    attend(up(0, 4))
+    attend(up(1, 4))
     pl.when(z >= 3)(finish)
 
     bcopy(WO, 0, 1 - k).wait_recv()
 
-    def rcopy(n, dx):
+    def rcopy(n, h, dx):
         there = (x + dx) % 4
         return pltpu.make_async_remote_copy(
-            src_ref=pbuf.at[n, :, there], dst_ref=rbuf.at[n, dx - 1], send_sem=rsend.at[0],
-            recv_sem=rrecv.at[n], device_id=(c, yh * 4 + there), device_id_type=MESH,
+            src_ref=pbuf.at[n, h, :, there], dst_ref=rbuf.at[n, h, dx - 1], send_sem=rsend.at[0],
+            recv_sem=rrecv.at[n, h], device_id=(c, yh * 4 + there), device_id_type=MESH,
         )
 
-    def pass_on(n):
-        acopy(0, 1, near[n]).wait_recv()
-        pl.when(inner)(lambda: acopy(1 + n, 2 if n == 1 else 1, near[n]).start())
-
-    def make_terms(n):
+    def pass_on(n, h):
+        acopy(0, 1, near[n], h).wait_recv()
+
+        @pl.when(inner)
+        def _():
+            acopy(1 + n, 2 if n == 1 else 1, near[n], h).start()
+
+    def make_terms(n, h):
         terms = lax.dot_general(
-            abuf[near[n]], wobuf[...].reshape(1024, 512), (((1,), (1,)), ((), ())),
+            abuf[near[n], pl.ds(h * HALF, HALF), :], wobuf[...].reshape(1024, 512), (((1,), (1,)), ((), ())),
             preferred_element_type=jnp.float32,
         ).astype(jnp.bfloat16)
         for slot in range(8):
-            pbuf[n, slot // 4, slot % 4] = terms[:, slot * HEAD:(slot + 1) * HEAD]
+            pbuf[n, h, slot // 4, slot % 4] = terms[:, slot * HEAD:(slot + 1) * HEAD]
         for dx in (2, 1, 3):
-            rcopy(n, dx).start()
-
-    def hcopy(n, j):
+            rcopy(n, h, dx).start()
+
+    def hcopy(n, h, j):
         half = (other, yh)[j]
         return pltpu.make_async_remote_copy(
-            src_ref=sbuf.at[n, j], dst_ref=ybuf.at[yh * 4 + y], send_sem=hsend.at[0], recv_sem=hrecv.at[0],
-            device_id=((z * NY + near[n]) * 2 + k, half * 4 + x), device_id_type=MESH,
+            src_ref=sbuf.at[n, h, j], dst_ref=ybuf.at[yh * 4 + y, pl.ds(h * HALF, HALF)], send_sem=hsend.at[0],
+            recv_sem=hrecv.at[0], device_id=((z * NY + near[n]) * 2 + k, half * 4 + x), device_id_type=MESH,
         )
 
-    def sum_over_x(n):
-        remote(rbuf.at[n], rsend.at[0], rrecv.at[n], sibling).wait_recv()
+    def sum_over_x(n, h):
+        remote(rbuf.at[n, h], rsend.at[0], rrecv.at[n, h], sibling).wait_recv()
         for j, half in ((0, other), (1, yh)):
-            total = pbuf[n, half, x].astype(jnp.float32)
+            total = pbuf[n, h, half, x].astype(jnp.float32)
             for dx in (1, 2, 3):
-                total = total + rbuf[n, dx - 1, half].astype(jnp.float32)
+                total = total + rbuf[n, h, dx - 1, half].astype(jnp.float32)
             if n == 0 and j == 1:
-                ybuf[yh * 4 + y] = total.astype(jnp.bfloat16)
+                ybuf[yh * 4 + y, pl.ds(h * HALF, HALF), :] = total.astype(jnp.bfloat16)
             else:
-                sbuf[n, j] = total.astype(jnp.bfloat16)
-                hcopy(n, j).start()
-
-    make_terms(0)
-    pass_on(1)
-    make_terms(1)
-    pass_on(2)
-    make_terms(2)
-    sum_over_x(0)
-    pass_on(3)
-    make_terms(3)
-    sum_over_x(1)
-    sum_over_x(2)
-    sum_over_x(3)
+                sbuf[n, h, j] = total.astype(jnp.bfloat16)
+                hcopy(n, h, j).start()
+
+    make_terms(0, 0)
+    make_terms(0, 1)
+    pass_on(1, 0)
+    make_terms(1, 0)
+    pass_on(2, 0)
+    pass_on(1, 1)
+    make_terms(1, 1)
+    pass_on(2, 1)
+    make_terms(2, 0)
+    sum_over_x(0, 0)
+    pass_on(3, 0)
+    make_terms(2, 1)
+    sum_over_x(0, 1)
+    make_terms(3, 0)
+    pass_on(3, 1)
+    make_terms(3, 1)
+    sum_over_x(1, 0)
+    sum_over_x(1, 1)
+    sum_over_x(2, 0)
+    sum_over_x(2, 1)
+    sum_over_x(3, 0)
+    sum_over_x(3, 1)
     for g in (WKV, WQ, KV, WO, WB):
         drain(g)
     remote(xbuf.at[pl.ds(0, 7)], tsend.at[0], orecv.at[0, 0], sibling).wait_send()
-    acopy(0, 1, y).wait_send()
+    remote(abuf.at[y], asend.at[0], orecv.at[0, 0], sibling).wait_send()
 
     @pl.when(inner)
     def _():
         for kind in (1, 2, 3, 4):
-            acopy(kind, 1, y).wait_send()
+            remote(abuf.at[y], asend.at[kind], orecv.at[0, 0], sibling).wait_send()
 
     remote(rbuf, rsend.at[0], orecv.at[0, 0], sibling).wait_send()
     remote(ybuf.at[pl.ds(0, 7)], hsend.at[0], hrecv.at[0], sibling).wait_send()
@@ -422,6 +457,10 @@
     vmem = pl.BlockSpec(memory_space=pltpu.VMEM)
     bf16, f32 = jnp.bfloat16, jnp.float32
     dma = pltpu.SemaphoreType.DMA
+    operands = [
+        pltpu.with_memory_space_constraint(a, pltpu.HBM)
+        for a in (tokens, w_query, key_matrix, value_matrix, w_out.T, table)
+    ]
     return pl.pallas_call(
         kernel,
         out_shape=jax.ShapeDtypeStruct((TOK, 512), bf16),
@@ -440,9 +479,9 @@
             pltpu.VMEM((HEADS * TOK, HEAD), f32),
             pltpu.VMEM((HEADS * TOK, HEAD), f32),
             pltpu.VMEM((NY, TOK, 512), bf16),
-            pltpu.VMEM((NY, 2, 4, TOK, HEAD), bf16),
-            pltpu.VMEM((NY, 3, 2, TOK, HEAD), bf16),
-            pltpu.VMEM((NY, 2, TOK, HEAD), bf16),
+            pltpu.VMEM((NY, 2, 2, 4, HALF, HEAD), bf16),
+            pltpu.VMEM((NY, 2, 3, 2, HALF, HEAD), bf16),
+            pltpu.VMEM((NY, 2, 2, HALF, HEAD), bf16),
             pltpu.VMEM((2 * NY, TOK, HEAD), bf16),
             dma((6,)),
             dma((5,)),
@@ -457,16 +496,16 @@
             dma((1,)),
             dma((NY,)),
             dma((5,)),
-            dma((NY,)),
+            dma((NY, 2)),
             dma((1,)),
-            dma((NY,)),
+            dma((NY, 2)),
             dma((1,)),
             dma((1,)),
         ],
         compiler_params=pltpu.CompilerParams(
-            collective_id=0, has_side_effects=True
+            collective_id=0, has_side_effects=True, vmem_limit_bytes=50 * 2**20
         ),
-    )(tokens, w_query, key_matrix, value_matrix, w_out.T, table)
+    )(*operands)
 
 
 def solution(mesh):

time: 98.7 us -> 94.5 us (0.957)
  Pallas kernels: 96 us -> 92.9 us
    pallas_call x1, Pallas kernels: 96 us -> 92.9 us  [body(): pl.pallas_call(kernel, out_shape=jax.ShapeDtypeStruct((TOK, 512), bf16),...]
where the time goes in v4:
time: 94.5 us; the launch traced here: 93.5 us
  Pallas kernels  92.9 us (98%)
    pallas_call x1, Pallas kernels, body(): pl.pallas_call(kernel, out_shape=jax.ShapeDtypeStruct((TOK, 512), bf16),...  92.9 us

profile of v4, /device:TPU:1, one launch (start us, length us, event | category | flops | bytes accessed | tf_op | source)
XLA Modules:
  0.0 93.5 jit_solution(9615398248263405095)
XLA Ops:
  0.0 92.9 %shard_map.64 = bf16[128,512]{1,0:T(8,128)(2,1)S(1)} custom-call(bf16[128,512]{1,0:T(8,128)(2,1)} %tok.1, bf16[64,512]{1,0:T(8,128)(2,1)} %wq.1, bf16[64,128]{1,0:T(8,128)(2,1)} %wk.1, bf16[64,128]{1,0:T(8,128)(2,1)} %wv.1, bf16[64,512]{1,0:T(8,128)(2,1)} %bitcast.1, f32[1,128]{1,0:T(1,128)} %constant.2.clone.invf), custom_call_target="tpu_custom_call" | custom-call | tf_op jit(solution)/shard_map/pallas_call | solution.py:464
  92.9 0.7 copy.8

commit v5 on v4

--- a/solution.py
+++ b/solution.py
@@ -17,14 +17,14 @@
 HALF = TOK // 2
 SCALE2 = math.log2(math.e) / math.sqrt(HEAD)
 REACH = ((4, 3), (3, 4))
-WKV, WQ, KV, WO, WB = 0, 1, 2, 3, 4
+WKV, WQ, KV, WO, WB, WP = 0, 1, 2, 3, 4, 5
 FIRST = 48
 
 
 def kernel(
     tok, wq, wk, wv, wo, invf, out,
     xbuf, wkvbuf, wqbuf, kvbuf, wobuf, table, qbuf, proj, mbuf, lbuf, acc, abuf, pbuf, rbuf, sbuf, ybuf,
-    local, zsend, ysend, bsend, zrecv, yrecv, brecv, orecv, tsend, trecv, lsend, lrecv, asend, arecv, rsend, rrecv, hsend, hrecv,
+    local, zsend, ysend, bsend, ksend, zrecv, yrecv, brecv, orecv, tsend, trecv, lsend, lrecv, osend, asend, arecv, rsend, rrecv, hsend, hrecv,
 ):
     c = lax.axis_index("ctx")
     f = lax.axis_index("fsdp")
@@ -60,7 +60,9 @@
 
     def pair(g, zz, p):
         if g == WO:
-            return wobuf.at[zz, k]
+            return wobuf.at[0, zz, k]
+        if g == WP:
+            return wobuf.at[1, zz, k]
         if g == WB:
             return late(zz, y, k)
         return view(g, zz, pl.ds(base[p], 2), k)
@@ -81,8 +83,14 @@
     sibling = at(z, y, 1 - k)
 
     def bcopy(g, zz, kk):
-        ref = wobuf.at[:, kk] if g == WO else late(slice(None), slice(None), kk) if g == WB else view(g, zz, slice(None), kk)
-        return remote(ref, bsend.at[g], brecv.at[g, zz], sibling)
+        ref = wobuf.at[g // WP, :, kk] if g in (WO, WP) else late(slice(None), slice(None), kk) if g == WB else view(g, zz, slice(None), kk)
+        return remote(ref, ksend.at[zz] if g == KV else bsend.at[g], brecv.at[g, zz], sibling)
+
+    def share(g, zz):
+        if g == KV:
+            pl.when(zz <= z)(lambda: bcopy(g, zz, k).start())
+        else:
+            bcopy(g, zz, k).start()
 
     def paired(g, zz):
         bcopy(g, zz, 1 - k).wait_recv()
@@ -120,18 +128,18 @@
                 if s < REACH[d][p]:
                     zcopy(g, d, s, p).start()
         if g < WO and last:
-            bcopy(g, up(1, s), k).start()
+            share(g, up(1, s))
             if s < 4:
-                bcopy(g, up(0, s), k).start()
-        elif s == 4 and g == WO:
+                share(g, up(0, s))
+        elif s == 4 and g in (WO, WP):
             bcopy(g, 0, k).start()
 
     def wcopy(n, yy):
         return remote(late(slice(None), yy, k), lsend.at[0], lrecv.at[yy], at(z, near[n], k))
 
     def drain(g):
-        if g == WO:
-            remote(wobuf.at[pl.ds(0, 7), k], zsend.at[g], orecv.at[0, 0], sibling).wait_send()
+        if g in (WO, WP):
+            remote(wobuf.at[0, pl.ds(0, 7), k], zsend.at[g], orecv.at[0, 0], sibling).wait_send()
             bcopy(g, 0, k).wait_send()
             return
         if g == WB:
@@ -141,7 +149,11 @@
             return
         remote(view(g, pl.ds(0, 7), slice(None), k), zsend.at[g], orecv.at[0, 0], sibling).wait_send()
         remote(view(g, 0, pl.ds(0, 3), k), ysend.at[g], orecv.at[0, 0], sibling).wait_send()
-        remote(view(g, slice(None), slice(None), k), bsend.at[g], orecv.at[0, 0], sibling).wait_send()
+        if g == KV:
+            for zz in range(NZ):
+                pl.when(zz <= z)(lambda: bcopy(g, zz, k).wait_send())
+        else:
+            remote(view(g, slice(None), slice(None), k), bsend.at[g], orecv.at[0, 0], sibling).wait_send()
 
     def tcopy(slot, peer):
         return remote(xbuf.at[slot], tsend.at[0], trecv.at[slot], (c, peer))
@@ -166,7 +178,7 @@
     copies = [
         pltpu.make_async_copy(wk, mine.at[:, pl.ds(0, HEAD)], local.at[0]),
         pltpu.make_async_copy(wv, mine.at[:, pl.ds(HEAD, HEAD)], local.at[1]),
-        pltpu.make_async_copy(wo, wobuf.at[z, k], local.at[2]),
+        pltpu.make_async_copy(wo, wobuf.at[0, z, k], local.at[2]),
         pltpu.make_async_copy(wq, wqbuf.at[z, y, k], local.at[3]),
         pltpu.make_async_copy(tok, xbuf.at[f], local.at[4]),
         pltpu.make_async_copy(invf, table, local.at[5]),
@@ -178,7 +190,7 @@
     peers = [at(up(0, 1), y, k), at(up(1, 1), y, k), at(z, y, 1 - k)]
     peers += [at(z, near[n], k) for n in (1, 2, 3)]
     peers += [(c, yh * 4 + (x + dx) % 4) for dx in (1, 2, 3)]
-    peers += [((z * NY + near[n]) * 2 + k, twin) for n in (0, 1, 2, 3)]
+    peers += [((z * NY + near[n]) * 2 + k, twin) for n in (0, 1)]
     for peer in peers:
         pl.semaphore_signal(barrier, inc=1, device_id=peer, device_id_type=MESH)
     for copy in copies:
@@ -202,6 +214,18 @@
 
     def turned(piece):
         return (piece * cosine + pltpu.roll(piece, HEAD // 2, 1) * sine).astype(jnp.bfloat16)
+
+    second = (y + 2) % NY
+
+    def second_copy():
+        return pltpu.make_async_remote_copy(
+            src_ref=wobuf.at[0, z, k], dst_ref=wobuf.at[1, z, k], send_sem=osend.at[0], recv_sem=osend.at[1],
+            device_id=at(z, second, k), device_id_type=MESH,
+        )
+
+    def take_second():
+        second_copy().wait_recv()
+        open_z(WP)
 
     def send_late():
         for n in (1, 2, 3):
@@ -236,13 +260,13 @@
         for h in range(HEADS):
             qbuf[pl.ds(h * TOK, TOK), :] = turned(proj[:, pl.ds(h * HEAD, HEAD)])
 
-    rows = 256
+    rows = 512
     keys = NY * 2 * TOK
 
     def attend(zz, first=False):
-        paired(KV, zz)
-
         def some():
+            paired(KV, zz)
+
             def body(i, carry):
                 at_rows = pl.ds(pl.multiple_of(i * rows, rows), rows)
                 key = kvbuf[zz, :, :, 0].reshape(keys, HEAD)
@@ -280,22 +304,19 @@
         else:
             pl.when(zz <= z)(some)
 
-    inner = jnp.logical_or(y == 1, y == 2)
-
-    def acopy(kind, n, yy, h):
-        ref = abuf.at[yy, pl.ds(h * HALF, HALF)]
-        return remote(ref, asend.at[kind], arecv.at[yy, h], at(z, near[n], k))
+    def acopy(h):
+        at_rows = pl.ds(h * HALF, HALF)
+        return pltpu.make_async_remote_copy(
+            src_ref=abuf.at[0, at_rows], dst_ref=abuf.at[1, at_rows], send_sem=asend.at[0], recv_sem=arecv.at[h],
+            device_id=at(z, near[1], k), device_id_type=MESH,
+        )
 
     def finish():
         for h in range(HEADS):
             at_rows = pl.ds(h * TOK, TOK)
-            abuf[y, :, pl.ds(h * HEAD, HEAD)] = (acc[at_rows, :] / lbuf[at_rows, :]).astype(jnp.bfloat16)
+            abuf[0, :, pl.ds(h * HEAD, HEAD)] = (acc[at_rows, :] / lbuf[at_rows, :]).astype(jnp.bfloat16)
         for h in (0, 1):
-            acopy(0, 1, y, h).start()
-
-            @pl.when(inner)
-            def _():
-                acopy(1, 2, y, h).start()
+            acopy(h).start()
 
     step0a(WKV, False)
     step(WB, 1, 0, True)
@@ -308,6 +329,7 @@
     step(WO, 2, 0, True)
     step0b(WQ, True)
     tcopy(*tokens_out[0]).start()
+    second_copy().start()
     step(WB, 3, 0, True)
     step(WKV, 2, 0, False)
     step(WKV, 2, 1, True)
@@ -319,7 +341,7 @@
     send_late()
     step(WKV, 3, 0, False)
     step(WKV, 3, 1, True)
-    step(WO, 4, 0, True)
+    take_second()
     step(WQ, 1, 0, False)
     step(WQ, 1, 1, True)
     tok_arrived(twin)
@@ -332,6 +354,7 @@
     step(WQ, 2, 0, False)
     step(WQ, 2, 1, True)
     make_keys()
+    step(WP, 1, 0, True)
     step(WQ, 3, 0, False)
     step(WQ, 3, 1, True)
     take_late()
@@ -341,6 +364,7 @@
     step(WQ, 4, 1, True)
     step(KV, 1, 0, False)
     step(KV, 1, 1, True)
+    step(WP, 2, 0, True)
     make_queries()
     attend(z, True)
     pl.when(z == 0)(finish)
@@ -351,96 +375,89 @@
     pl.when(z == 1)(finish)
     step(KV, 3, 0, False)
     step(KV, 3, 1, True)
+    step(WP, 3, 0, True)
     attend(up(1, 2))
     attend(up(0, 2))
     pl.when(z == 2)(finish)
-    step(KV, 4, 0, False)
-    step(KV, 4, 1, True)
+    pl.when(z >= 4)(lambda: step(KV, 4, 0, False))
+    pl.when(z >= 4)(lambda: step(KV, 4, 1, True))
+    step(WO, 4, 0, True)
     attend(up(1, 3))
     attend(up(0, 3))
     attend(up(1, 4))
     pl.when(z >= 3)(finish)
 
-    bcopy(WO, 0, 1 - k).wait_recv()
-
-    def rcopy(n, h, dx):
+    def rcopy(q, n, h, dx):
         there = (x + dx) % 4
         return pltpu.make_async_remote_copy(
-            src_ref=pbuf.at[n, h, :, there], dst_ref=rbuf.at[n, h, dx - 1], send_sem=rsend.at[0],
-            recv_sem=rrecv.at[n, h], device_id=(c, yh * 4 + there), device_id_type=MESH,
+            src_ref=pbuf.at[q, n, h, :, there], dst_ref=rbuf.at[q, n, h, dx - 1], send_sem=rsend.at[0],
+            recv_sem=rrecv.at[q, n, h], device_id=(c, yh * 4 + there), device_id_type=MESH,
         )
 
-    def pass_on(n, h):
-        acopy(0, 1, near[n], h).wait_recv()
-
-        @pl.when(inner)
-        def _():
-            acopy(1 + n, 2 if n == 1 else 1, near[n], h).start()
-
-    def make_terms(n, h):
+    def make_terms(q, n, h):
         terms = lax.dot_general(
-            abuf[near[n], pl.ds(h * HALF, HALF), :], wobuf[...].reshape(1024, 512), (((1,), (1,)), ((), ())),
+            abuf[n, pl.ds(h * HALF, HALF), :], wobuf[q].reshape(1024, 512), (((1,), (1,)), ((), ())),
             preferred_element_type=jnp.float32,
         ).astype(jnp.bfloat16)
         for slot in range(8):
-            pbuf[n, h, slot // 4, slot % 4] = terms[:, slot * HEAD:(slot + 1) * HEAD]
+            pbuf[q, n, h, slot // 4, slot % 4] = terms[:, slot * HEAD:(slot + 1) * HEAD]
         for dx in (2, 1, 3):
-            rcopy(n, h, dx).start()
-
-    def hcopy(n, h, j):
+            rcopy(q, n, h, dx).start()
+
+    def hcopy(q, n, h, j):
         half = (other, yh)[j]
         return pltpu.make_async_remote_copy(
-            src_ref=sbuf.at[n, h, j], dst_ref=ybuf.at[yh * 4 + y, pl.ds(h * HALF, HALF)], send_sem=hsend.at[0],
-            recv_sem=hrecv.at[0], device_id=((z * NY + near[n]) * 2 + k, half * 4 + x), device_id_type=MESH,
+            src_ref=sbuf.at[q, n, h, j], dst_ref=ybuf.at[yh * 4 + (y, second)[q], pl.ds(h * HALF, HALF)],
+            send_sem=hsend.at[0], recv_sem=hrecv.at[0],
+            device_id=((z * NY + near[n]) * 2 + k, half * 4 + x), device_id_type=MESH,
         )
 
-    def sum_over_x(n, h):
-        remote(rbuf.at[n, h], rsend.at[0], rrecv.at[n, h], sibling).wait_recv()
+    def sum_over_x(q, n, h):
+        remote(rbuf.at[q, n, h], rsend.at[0], rrecv.at[q, n, h], sibling).wait_recv()
         for j, half in ((0, other), (1, yh)):
-            total = pbuf[n, h, half, x].astype(jnp.float32)
+            total = pbuf[q, n, h, half, x].astype(jnp.float32)
             for dx in (1, 2, 3):
-                total = total + rbuf[n, h, dx - 1, half].astype(jnp.float32)
+                total = total + rbuf[q, n, h, dx - 1, half].astype(jnp.float32)
             if n == 0 and j == 1:
-                ybuf[yh * 4 + y, pl.ds(h * HALF, HALF), :] = total.astype(jnp.bfloat16)
+                ybuf[yh * 4 + (y, second)[q], pl.ds(h * HALF, HALF), :] = total.astype(jnp.bfloat16)
             else:
-                sbuf[n, h, j] = total.astype(jnp.bfloat16)
-                hcopy(n, h, j).start()
-
-    make_terms(0, 0)
-    make_terms(0, 1)
-    pass_on(1, 0)
-    make_terms(1, 0)
-    pass_on(2, 0)
-    pass_on(1, 1)
-    make_terms(1, 1)
-    pass_on(2, 1)
-    make_terms(2, 0)
-    sum_over_x(0, 0)
-    pass_on(3, 0)
-    make_terms(2, 1)
-    sum_over_x(0, 1)
-    make_terms(3, 0)
-    pass_on(3, 1)
-    make_terms(3, 1)
-    sum_over_x(1, 0)
-    sum_over_x(1, 1)
-    sum_over_x(2, 0)
-    sum_over_x(2, 1)
-    sum_over_x(3, 0)
-    sum_over_x(3, 1)
-    for g in (WKV, WQ, KV, WO, WB):
+                sbuf[q, n, h, j] = total.astype(jnp.bfloat16)
+                hcopy(q, n, h, j).start()
+
+    bcopy(WO, 0, 1 - k).wait_recv()
+    make_terms(0, 0, 0)
+    make_terms(0, 0, 1)
+    step(WP, 4, 0, True)
+    acopy(0).wait_recv()
+    make_terms(0, 1, 0)
+    acopy(1).wait_recv()
+    make_terms(0, 1, 1)
+    sum_over_x(0, 0, 0)
+    bcopy(WP, 0, 1 - k).wait_recv()
+    make_terms(1, 0, 0)
+    sum_over_x(0, 0, 1)
+    make_terms(1, 0, 1)
+    make_terms(1, 1, 0)
+    make_terms(1, 1, 1)
+    sum_over_x(0, 1, 0)
+    sum_over_x(0, 1, 1)
+    sum_over_x(1, 0, 0)
+    sum_over_x(1, 0, 1)
+    sum_over_x(1, 1, 0)
+    sum_over_x(1, 1, 1)
+    @pl.when(z < 4)
+    def _():
+        step(KV, 4, 0, False)
+        step(KV, 4, 1, True)
+
+    for g in (WKV, WQ, KV, WO, WB, WP):
         drain(g)
     remote(xbuf.at[pl.ds(0, 7)], tsend.at[0], orecv.at[0, 0], sibling).wait_send()
-    remote(abuf.at[y], asend.at[0], orecv.at[0, 0], sibling).wait_send()
-
-    @pl.when(inner)
-    def _():
-        for kind in (1, 2, 3, 4):
-            remote(abuf.at[y], asend.at[kind], orecv.at[0, 0], sibling).wait_send()
-
+    remote(abuf.at[0], asend.at[0], orecv.at[0, 0], sibling).wait_send()
+    second_copy().wait_send()
     remote(rbuf, rsend.at[0], orecv.at[0, 0], sibling).wait_send()
-    remote(ybuf.at[pl.ds(0, 7)], hsend.at[0], hrecv.at[0], sibling).wait_send()
-    remote(ybuf.at[pl.ds(0, 7)], hsend.at[0], hrecv.at[0], sibling).wait_recv()
+    remote(ybuf.at[pl.ds(0, 6)], hsend.at[0], hrecv.at[0], sibling).wait_send()
+    remote(ybuf.at[pl.ds(0, 6)], hsend.at[0], hrecv.at[0], sibling).wait_recv()
     for n in range(NY):
         out[:, pl.ds(n * HEAD, HEAD)] = (
             ybuf[n].astype(jnp.float32) + ybuf[4 + n].astype(jnp.float32)
@@ -471,34 +488,36 @@
             pltpu.VMEM((NZ, NY, 2, 64, 2 * HEAD), bf16),
             pltpu.VMEM((NZ, NY, 2, 64, 512), bf16),
             pltpu.VMEM((NZ, NY, 2, 2, TOK, HEAD), bf16),
-            pltpu.VMEM((NZ, 2, 64, 512), bf16),
+            pltpu.VMEM((2, NZ, 2, 64, 512), bf16),
             pltpu.VMEM((1, HEAD), f32),
             pltpu.VMEM((HEADS * TOK, HEAD), bf16),
             pltpu.VMEM((TOK, 512), f32),
             pltpu.VMEM((HEADS * TOK, HEAD), f32),
             pltpu.VMEM((HEADS * TOK, HEAD), f32),
             pltpu.VMEM((HEADS * TOK, HEAD), f32),
-            pltpu.VMEM((NY, TOK, 512), bf16),
-            pltpu.VMEM((NY, 2, 2, 4, HALF, HEAD), bf16),
-            pltpu.VMEM((NY, 2, 3, 2, HALF, HEAD), bf16),
-            pltpu.VMEM((NY, 2, 2, HALF, HEAD), bf16),
+            pltpu.VMEM((2, TOK, 512), bf16),
+            pltpu.VMEM((2, 2, 2, 2, 4, HALF, HEAD), bf16),
+            pltpu.VMEM((2, 2, 2, 3, 2, HALF, HEAD), bf16),
+            pltpu.VMEM((2, 2, 2, 2, HALF, HEAD), bf16),
             pltpu.VMEM((2 * NY, TOK, HEAD), bf16),
             dma((6,)),
-            dma((5,)),
+            dma((6,)),
             dma((3,)),
-            dma((5,)),
+            dma((6,)),
+            dma((NZ,)),
             dma((3, NZ, 2)),
             dma((3, 2)),
-            dma((5, NZ)),
-            dma((2, NZ)),
+            dma((6, NZ)),
+            dma((3, NZ)),
             dma((1,)),
             dma((8,)),
             dma((1,)),
             dma((NY,)),
-            dma((5,)),
-            dma((NY, 2)),
+            dma((2,)),
             dma((1,)),
-            dma((NY, 2)),
+            dma((2,)),
+            dma((1,)),
+            dma((2, 2, 2)),
             dma((1,)),
             dma((1,)),
         ],

time: 94.5 us -> 91.9 us (0.972)
  Pallas kernels: 92.9 us -> 91.1 us
    pallas_call x1, Pallas kernels: 92.9 us -> 91.1 us  [body(): pl.pallas_call(kernel, out_shape=jax.ShapeDtypeStruct((TOK, 512), bf16),...]
where the time goes in v5:
time: 91.9 us; the launch traced here: 91.8 us
  Pallas kernels  91.1 us (99%)
    pallas_call x1, Pallas kernels, body(): pl.pallas_call(kernel, out_shape=jax.ShapeDtypeStruct((TOK, 512), bf16),...  91.1 us

profile of v5, /device:TPU:1, one launch (start us, length us, event | category | flops | bytes accessed | tf_op | source)
XLA Modules:
  0.0 91.8 jit_solution(1867120677814166534)
XLA Ops:
  0.0 91.1 %shard_map.64 = bf16[128,512]{1,0:T(8,128)(2,1)S(1)} custom-call(bf16[128,512]{1,0:T(8,128)(2,1)} %tok.1, bf16[64,512]{1,0:T(8,128)(2,1)} %wq.1, bf16[64,128]{1,0:T(8,128)(2,1)} %wk.1, bf16[64,128]{1,0:T(8,128)(2,1)} %wv.1, bf16[64,512]{1,0:T(8,128)(2,1)} %bitcast.1, f32[1,128]{1,0:T(1,128)} %constant.2.clone.invf), custom_call_target="tpu_custom_call" | custom-call | tf_op jit(solution)/shard_map/pallas_call | solution.py:481
  91.1 0.7 copy.8

commit v6 on v5

--- a/solution.py
+++ b/solution.py
@@ -355,6 +355,7 @@
     step(WQ, 2, 1, True)
     make_keys()
     step(WP, 1, 0, True)
+    step(WO, 4, 0, True)
     step(WQ, 3, 0, False)
     step(WQ, 3, 1, True)
     take_late()
@@ -379,11 +380,10 @@
     attend(up(1, 2))
     attend(up(0, 2))
     pl.when(z == 2)(finish)
+    attend(up(1, 3))
+    attend(up(0, 3))
     pl.when(z >= 4)(lambda: step(KV, 4, 0, False))
     pl.when(z >= 4)(lambda: step(KV, 4, 1, True))
-    step(WO, 4, 0, True)
-    attend(up(1, 3))
-    attend(up(0, 3))
     attend(up(1, 4))
     pl.when(z >= 3)(finish)
 

time: 91.9 us -> 90.4 us (0.984)
  Pallas kernels: 91.1 us -> 89.6 us
    pallas_call x1, Pallas kernels: 91.1 us -> 89.6 us  [body(): pl.pallas_call(kernel, out_shape=jax.ShapeDtypeStruct((TOK, 512), bf16),...]
where the time goes in v6:
time: 90.4 us; the launch traced here: 90.2 us
  Pallas kernels  89.6 us (99%)
    pallas_call x1, Pallas kernels, body(): pl.pallas_call(kernel, out_shape=jax.ShapeDtypeStruct((TOK, 512), bf16),...  89.6 us

profile of v6, /device:TPU:1, one launch (start us, length us, event | category | flops | bytes accessed | tf_op | source)
XLA Modules:
  0.0 90.2 jit_solution(16783937672233453893)
XLA Ops:
  0.0 89.6 %shard_map.64 = bf16[128,512]{1,0:T(8,128)(2,1)S(1)} custom-call(bf16[128,512]{1,0:T(8,128)(2,1)} %tok.1, bf16[64,512]{1,0:T(8,128)(2,1)} %wq.1, bf16[64,128]{1,0:T(8,128)(2,1)} %wk.1, bf16[64,128]{1,0:T(8,128)(2,1)} %wv.1, bf16[64,512]{1,0:T(8,128)(2,1)} %bitcast.1, f32[1,128]{1,0:T(1,128)} %constant.2.clone.invf), custom_call_target="tpu_custom_call" | custom-call | tf_op jit(solution)/shard_map/pallas_call | solution.py:481
  89.6 0.7 copy.8

commit v7 on v6

--- a/solution.py
+++ b/solution.py
@@ -365,12 +365,12 @@
     step(WQ, 4, 1, True)
     step(KV, 1, 0, False)
     step(KV, 1, 1, True)
-    step(WP, 2, 0, True)
     make_queries()
     attend(z, True)
     pl.when(z == 0)(finish)
     step(KV, 2, 0, False)
     step(KV, 2, 1, True)
+    step(WP, 2, 0, True)
     attend(up(1, 1))
     attend(up(0, 1))
     pl.when(z == 1)(finish)

time: 90.4 us -> 90.4 us (level)
  no operation moved by 1% of the time
where the time goes in v7:
time: 90.4 us; the launch traced here: 89.7 us
  Pallas kernels  89 us (98%)
    pallas_call x1, Pallas kernels, body(): pl.pallas_call(kernel, out_shape=jax.ShapeDtypeStruct((TOK, 512), bf16),...  89 us

profile of v7, /device:TPU:1, one launch (start us, length us, event | category | flops | bytes accessed | tf_op | source)
XLA Modules:
  0.0 89.7 jit_solution(365382413863102006)
XLA Ops:
  0.0 89.0 %shard_map.64 = bf16[128,512]{1,0:T(8,128)(2,1)S(1)} custom-call(bf16[128,512]{1,0:T(8,128)(2,1)} %tok.1, bf16[64,512]{1,0:T(8,128)(2,1)} %wq.1, bf16[64,128]{1,0:T(8,128)(2,1)} %wk.1, bf16[64,128]{1,0:T(8,128)(2,1)} %wv.1, bf16[64,512]{1,0:T(8,128)(2,1)} %bitcast.1, f32[1,128]{1,0:T(1,128)} %constant.2.clone.invf), custom_call_target="tpu_custom_call" | custom-call | tf_op jit(solution)/shard_map/pallas_call | solution.py:481
  89.1 0.7 copy.8
